TPU v7x, 32 devices: a whole 2x2x4 slice. The times are simulated.
32 devices in a mesh: band: 8 (over z, x), tile: 4 (over y, core).
Axes of the slice: x: 2, y: 2, z: 4, core: 2. Of those that a mesh axis runs over, the one named last changes fastest.
Arguments:
- source: bfloat16 [40, 262144], P(None, ('band', 'tile')), may hold values from -6 to 6
- regrid_weights: bfloat16 [2048, 4, 128, 128], P(('band', 'tile')), may hold values from -0.5 to 0.5
- dest_group: int32 [2048, 4], P(('band', 'tile')), may hold values from 0 to 31, all different within a row; in each aligned block of 64 rows (0 to 63, 64 to 127, ...) at most 24 rows name the same one
- dest_block: int32 [2048, 4], P(('band', 'tile')), may hold values from 0 to 767
- seam_table: int32 [12, 4, 3], replicated, may hold values from 0 to 11, as said below
- conv1_weight: bfloat16 [9, 128, 40], replicated, may hold values from -0.3125 to 0.3125
- conv1_bias: float32 [128], replicated, may hold values from -3 to 3
- conv2_weight: bfloat16 [9, 128, 128], replicated, may hold values from -0.1875 to 0.1875
- conv2_bias: float32 [128], replicated, may hold values from -3 to 3
Outputs:
- features: bfloat16 [128, 12, 512, 512], P(None, None, 'band', 'tile')
Inputs may be any that keep to these rules, and one draw needn't show every extreme that they name: `dest_group`: within the rows of one device (aligned blocks of 64 rows) no value appears more than 24 times, and a row's 4 values differ. `seam_table`: entries 0 and 1 name a face and a side (0 to 3). Joins are symmetric: if side s of face f is joined to side s2 of face g, side s2 of face g is joined to side s of face f with the same reversal entry. No side is joined to itself. Entry 2 is 0 or 1.
All inputs are finite; a program needn't handle non-finite values.
Results may differ from a plain program's by a relative error of at most 0.0058.
Values may be sent and summed in bfloat16 or wider, within the bound.
A program may use at most 640 MiB of HBM per device.

v0:
```python
import functools

import jax
import jax.numpy as jnp
from jax import lax
from jax.experimental import pallas as pl
from jax.experimental.pallas import tpu as pltpu
from jax.sharding import PartitionSpec as P

BF = jnp.bfloat16
F32 = jnp.float32
VMEM_LIMIT = 60 * 1024 * 1024
PAIRS = 8
UNROLLED = True
GELU_COEF = (
    0.7978842684146765,
    0.03633414911622174,
    -3.30267008968913e-05,
    -5.527338755532785e-05,
    3.974071022505988e-06,
    -1.3378322650770525e-07,
    1.8139281733930472e-09,
)
GELU_CAP = 30.0


def gelu(v):
    u = jnp.minimum(v * v, GELU_CAP)
    q = jnp.full_like(u, GELU_COEF[-1])
    for c in GELU_COEF[-2::-1]:
        q = q * u + c
    half = 0.5 * v
    return half + half * jnp.tanh(v * q)


def partial_kernel(pos_ref, src_ref, w_ref, out_ref):
    s = pl.program_id(0)
    per_step = w_ref.shape[0]
    top, blk = w_ref.shape[1], w_ref.shape[2]

    @pl.when(s == 0)
    def _():
        out_ref[...] = jnp.zeros_like(out_ref)

    for j in range(per_step):
        x = src_ref[:, j * blk : (j + 1) * blk]
        for k in range(top):
            y = jnp.dot(x, w_ref[j, k], preferred_element_type=F32).astype(BF)
            out_ref[pos_ref[(s * per_step + j) * top + k]] = y


def partials(position, source, weights, slots):
    fields = source.shape[0]
    src_count, top, blk, _ = weights.shape
    step = 4
    return pl.pallas_call(
        partial_kernel,
        out_shape=jax.ShapeDtypeStruct((slots, fields, blk), BF),
        grid_spec=pltpu.PrefetchScalarGridSpec(
            num_scalar_prefetch=1,
            grid=(src_count // step,),
            in_specs=[
                pl.BlockSpec((fields, step * blk), lambda i, p: (0, i)),
                pl.BlockSpec((step, top, blk, blk), lambda i, p: (i, 0, 0, 0)),
            ],
            out_specs=pl.BlockSpec((slots, fields, blk), lambda i, p: (0, 0, 0)),
        ),
        compiler_params=pltpu.CompilerParams(vmem_limit_bytes=VMEM_LIMIT),
        name="partials",
    )(position, source, weights)


def collect_kernel(slot_ref, arr_ref, out_ref, acc_ref):
    i = pl.program_id(0)
    n = arr_ref.shape[0]

    @pl.when(i == 0)
    def _():
        acc_ref[...] = jnp.zeros_like(acc_ref)

    def body(j, _):
        slot = slot_ref[i * n + j]
        acc_ref[slot] = acc_ref[slot] + arr_ref[j].astype(F32)
        return 0

    lax.fori_loop(0, n, body, 0, unroll=4)

    @pl.when(i == pl.num_programs(0) - 1)
    def _():
        out_ref[...] = acc_ref[: out_ref.shape[0]].astype(BF)


def collect(slots, arrived, slots_dev):
    count, fields, blk = arrived.shape
    steps = 8
    return pl.pallas_call(
        collect_kernel,
        out_shape=jax.ShapeDtypeStruct((slots_dev, fields, blk), BF),
        grid_spec=pltpu.PrefetchScalarGridSpec(
            num_scalar_prefetch=1,
            grid=(steps,),
            in_specs=[pl.BlockSpec((count // steps, fields, blk), lambda i, p: (i, 0, 0))],
            out_specs=pl.BlockSpec((slots_dev, fields, blk), lambda i, p: (0, 0, 0)),
            scratch_shapes=[pltpu.VMEM((slots_dev + 1, fields, blk), F32)],
        ),
        compiler_params=pltpu.CompilerParams(vmem_limit_bytes=VMEM_LIMIT),
        name="collect",
    )(slots, arrived)


def conv_kernel(
    first, x_ref, top_ref, bot_ref, left_ref, right_ref, wa_ref, wb_ref, b_ref, out_ref, *scratch
):
    if first:
        ends, scratch = scratch[0], scratch[1:]
    sl, win = scratch[0], scratch[1]
    rows = out_ref.shape[0] if first else out_ref.shape[2]
    cols = sl.shape[1]
    width = sl.shape[2] // 2
    chan = left_ref.shape[-1]
    slots = win.shape[0]

    def put(slot, pair, parity, row32, lo, hi):
        win[slot, 8 : 8 + cols, :] = row32
        win[slot, 7:8, :] = lo
        win[slot, 8 + cols : 9 + cols, :] = hi
        before = win[slot, 7 : 7 + cols, :]
        after = win[slot, 9 : 9 + cols, :]
        base = parity * width
        if first:
            g = before + pltpu.roll(row32, chan, 1) + pltpu.roll(after, 2 * chan, 1)
            sl[pair, :, base : base + width] = g.astype(BF)
        else:
            sl[pair, :, base : base + cols] = before.astype(BF)
            sl[pair, :, base + cols : base + 2 * cols] = row32.astype(BF)
            sl[pair, :, base + 2 * cols : base + 3 * cols] = after.astype(BF)

    def wide(v):
        if first:
            v = jnp.concatenate([v, jnp.zeros((v.shape[0], cols - chan), v.dtype)], axis=1)
        return v

    def row_at(r):
        if first:
            y = x_ref[r].astype(F32)
            y = jnp.concatenate([y, jnp.zeros((cols - chan, cols), F32)], axis=0)
            return y.T
        return x_ref[r].astype(F32)

    def halo_row(ref):
        full = wide(ref[0].astype(F32))
        return full[:cols], full[cols : cols + 1], full[cols + 1 : cols + 2]

    def put_row(r, k):
        put(
            k % slots,
            r // 2 + k % 2 if isinstance(r, int) else (r - k % 2) // 2 + k % 2,
            1 - k % 2,
            row_at(r),
            wide(left_ref[0, pl.ds(r, 1), :]),
            wide(right_ref[0, pl.ds(r, 1), :]),
        )

    row, lo, hi = halo_row(top_ref)
    put(0, 0, 0, row, lo, hi)
    row, lo, hi = halo_row(bot_ref)
    put(1, rows // 2, 1, row, lo, hi)
    unroll = UNROLLED
    n = 2 * PAIRS

    def fill_loop(i, _):
        for k in range(slots):
            put_row(i * slots + k, k)
        return 0

    def dots(p0):
        a = sl[pl.ds(p0, PAIRS)].reshape(PAIRS * cols, 2 * width)
        b = sl[pl.ds(p0 + 1, PAIRS)].reshape(PAIRS * cols, 2 * width)
        return jnp.dot(a, wa_ref[...], preferred_element_type=F32) + jnp.dot(
            b, wb_ref[...], preferred_element_type=F32
        )

    def finish(g, y):
        p0 = g * PAIRS
        hid = y.shape[1] // 2
        if first:
            y = gelu(y + b_ref[...])
            for p in range(PAIRS):
                for q in range(2):
                    part = y[p * cols : (p + 1) * cols, q * hid : (q + 1) * hid].astype(BF)
                    r = 2 * (p0 + p) + q
                    out_ref[r] = part
                    ends[0, 0, pl.ds(r, 1), :] = part[:1].astype(F32)
                    ends[1, 0, pl.ds(r, 1), :] = part[cols - 1 :].astype(F32)
            return
        flip = scratch[2].at[g % 2 if unroll else 0]
        for p in range(PAIRS):
            for q in range(2):
                part = y[p * cols : (p + 1) * cols, q * hid : (q + 1) * hid]
                flip[pl.ds(2 * p + q, hid, stride=n), :] = part.T

        def group(o, _):
            for j in range(8):
                v = flip[pl.ds((o * 8 + j) * n, n), :]
                out_ref[o * 8 + j, 0, pl.ds(g * n, n), :] = gelu(v + b_ref[o * 8 + j]).astype(BF)
            return 0

        if unroll:
            for o in range(hid // 8):
                group(o, 0)
        else:
            lax.fori_loop(0, hid // 8, group, 0)

    if unroll:
        for k in range(min(n + 2, rows)):
            put_row(k, k)
        for g in range(rows // n):
            y = dots(g * PAIRS)
            for k in range((g + 1) * n + 2, min((g + 2) * n + 2, rows)):
                put_row(k, k)
            finish(g, y)
    else:
        lax.fori_loop(0, rows // slots, fill_loop, 0)

        def chunk(g, _):
            finish(g, dots(g * PAIRS))
            return 0

        lax.fori_loop(0, rows // n, chunk, 0)


def conv(first, x, halos, weight, bias, face_count, rows, out_cols):
    top, bot, left, right = halos
    hid, chan = weight.shape[1], weight.shape[2]
    cols = out_cols
    w = weight.reshape(3, 3, hid, chan).transpose(0, 1, 3, 2)
    if first:
        w = w.reshape(3, 3 * chan, hid)
        w = jnp.pad(w, ((0, 0), (0, cols - 3 * chan), (0, 0)))
    else:
        w = w.reshape(3, 3 * chan, hid)
    width = w.shape[1]
    zero = jnp.zeros((width, hid), w.dtype)
    wide = [
        jnp.concatenate([w[a] if a < 3 else zero, w[a - 1] if a > 0 else zero], axis=1)
        for a in range(4)
    ]
    wa = jnp.concatenate(wide[:2], axis=0)
    wb = jnp.concatenate(wide[2:], axis=0)
    scratch = [
        pltpu.VMEM((rows // 2 + 1, cols, 2 * width), BF),
        pltpu.VMEM((8, cols + 16, cols), F32),
    ]
    if first:
        bias_in = jnp.concatenate([bias, bias])[None, :]
        bias_spec = pl.BlockSpec((1, 2 * hid), lambda f: (0, 0))
        out_shape = (
            jax.ShapeDtypeStruct((face_count * rows, cols, hid), BF),
            jax.ShapeDtypeStruct((2, face_count, rows, hid), F32),
        )
        out_spec = (
            pl.BlockSpec((rows, cols, hid), lambda f: (f, 0, 0)),
            pl.BlockSpec((2, 1, rows, hid), lambda f: (0, f, 0, 0)),
        )
    else:
        bias_in = bias
        bias_spec = pl.BlockSpec(memory_space=pltpu.SMEM)
        out_shape = jax.ShapeDtypeStruct((hid, face_count, rows, cols), BF)
        out_spec = pl.BlockSpec((hid, 1, rows, cols), lambda f: (0, f, 0, 0))
        scratch.append(pltpu.VMEM((2, hid * 2 * PAIRS, cols), F32))
    return pl.pallas_call(
        functools.partial(conv_kernel, first),
        out_shape=out_shape,
        grid=(face_count,),
        in_specs=[
            pl.BlockSpec((rows,) + x.shape[1:], lambda f: (f, 0, 0)),
            pl.BlockSpec((1,) + top.shape[1:], lambda f: (f, 0, 0)),
            pl.BlockSpec((1,) + bot.shape[1:], lambda f: (f, 0, 0)),
            pl.BlockSpec((1,) + left.shape[1:], lambda f: (f, 0, 0)),
            pl.BlockSpec((1,) + right.shape[1:], lambda f: (f, 0, 0)),
            pl.BlockSpec(wa.shape, lambda f: (0, 0)),
            pl.BlockSpec(wb.shape, lambda f: (0, 0)),
            bias_spec,
        ],
        out_specs=out_spec,
        scratch_shapes=scratch,
        compiler_params=pltpu.CompilerParams(vmem_limit_bytes=VMEM_LIMIT),
        name="conv1" if first else "conv2",
    )(x, top, bot, left, right, wa, wb, bias_in)


def halos_of(top, bottom, left, right, seam_table):
    faces, cols, chan = top.shape
    rows = left.shape[1]
    nb, nt = lax.axis_size("band"), lax.axis_size("tile")
    band, tile = lax.axis_index("band"), lax.axis_index("tile")
    side = cols * nt

    row_edge = jnp.where(band == 0, top, bottom).reshape(nb, faces * cols // nb, chan)
    col_edge = jnp.where(tile == 0, left, right).reshape(nt, faces * rows // nt, chan)
    row_part = lax.all_to_all(row_edge, "band", 0, 0, tiled=True)
    col_part = lax.all_to_all(col_edge, "tile", 0, 0, tiled=True)
    mine = jnp.concatenate([row_part[0], row_part[-1], col_part[0], col_part[-1]], axis=0)
    every = lax.all_gather(mine, ("band", "tile"), axis=0, tiled=False)
    pieces = every.reshape(-1, rows, chan)
    per_row, per_col = row_edge.shape[1] // rows, col_edge.shape[1] // rows
    per_dev = 2 * (per_row + per_col)
    per_tile = cols // rows
    last_piece = side // rows - 1

    def wanted(which, first, count):
        at = first - 1 + jnp.arange(count + 2, dtype=jnp.int32)
        face = seam_table[:, which, 0][:, None]
        edge = seam_table[:, which, 1][:, None]
        rev = seam_table[:, which, 2][:, None] == 1
        q = jnp.clip(jnp.where(rev, last_piece - at, at), 0, last_piece)
        c = face * per_tile + q % per_tile
        on_row = (c // per_row * nt + q // per_tile) * per_dev + edge * per_row + c % per_row
        on_col = (
            (q * nt + face // per_col) * per_dev
            + 2 * per_row
            + (edge - 2) * per_col
            + face % per_col
        )
        return jnp.where(edge < 2, on_row, on_col), jnp.broadcast_to(rev, q.shape)

    asked = [
        (0, tile * per_tile, per_tile),
        (1, tile * per_tile, per_tile),
        (2, band, 1),
        (3, band, 1),
    ]
    parts = [wanted(*a) for a in asked]
    index = jnp.concatenate([p[0] for p in parts], axis=1)
    rev = jnp.concatenate([p[1] for p in parts], axis=1)
    got = jnp.take(pieces, index.reshape(-1), axis=0, mode="clip")
    flip = jnp.eye(rows, dtype=BF)[::-1]
    flipped = jnp.einsum("pq,kqc->kpc", flip, got, preferred_element_type=F32).astype(BF)
    got = jnp.where(rev.reshape(-1)[:, None, None], flipped, got)
    got = got.reshape(faces, index.shape[1], rows, chan)
    offset = [0]
    for a in asked:
        offset.append(offset[-1] + a[2] + 2)

    def segments(which):
        o, n, first = offset[which], asked[which][2], asked[which][1]
        middle = got[:, o + 1 : o + 1 + n].reshape(faces, n * rows, chan)
        lead = jnp.where(first > 0, got[:, o, -1:], 0)
        trail = jnp.where(first + n <= last_piece, got[:, o + 1 + n, :1], 0)
        return lead, middle, trail

    def shift(x, axis, size, forward):
        pairs = [(i, i + 1) if forward else (i + 1, i) for i in range(size - 1)]
        return lax.ppermute(x, axis, pairs)

    above = shift(bottom, "band", nb, True)
    below = shift(top, "band", nb, False)
    ext_left = jnp.concatenate([above[:, :1], left, below[:, :1]], axis=1)
    ext_right = jnp.concatenate([above[:, -1:], right, below[:, -1:]], axis=1)
    from_left = shift(ext_right, "tile", nt, True)
    from_right = shift(ext_left, "tile", nt, False)
    lefts = jnp.where(tile == 0, jnp.concatenate(segments(2), axis=1), from_left)
    rights = jnp.where(tile == nt - 1, jnp.concatenate(segments(3), axis=1), from_right)

    def line(at_edge, which, inner, at):
        lead, middle, trail = segments(which)
        lead = jnp.where(at_edge, lead, lefts[:, at : at + 1])
        trail = jnp.where(at_edge, trail, rights[:, at : at + 1])
        return jnp.concatenate([jnp.where(at_edge, middle, inner), lead, trail], axis=1)

    tops = line(band == 0, 0, above, 0)
    bots = line(band == nb - 1, 1, below, rows + 1)
    return tops, bots, lefts[:, 1:-1].astype(F32), rights[:, 1:-1].astype(F32)


def local(
    source,
    regrid_weights,
    dest_group,
    dest_block,
    seam_table,
    conv1_weight,
    conv1_bias,
    conv2_weight,
    conv2_bias,
):
    fields = source.shape[0]
    src_count, top_count, block_len, _ = regrid_weights.shape
    nb, nt = lax.axis_size("band"), lax.axis_size("tile")
    devices = nb * nt
    capacity = 3 * src_count * top_count // devices
    rows = block_len * nt // nb
    faces = seam_table.shape[0]
    slots_dev = faces * rows
    items = src_count * top_count
    target_dev = dest_group.reshape(items)
    target_slot = dest_block.reshape(items)
    onehot = (target_dev[:, None] == jnp.arange(devices, dtype=jnp.int32)[None, :]).astype(F32)
    earlier = (jnp.arange(items)[:, None] > jnp.arange(items)[None, :]).astype(BF)
    before = jnp.dot(earlier, onehot.astype(BF), preferred_element_type=F32)
    rank_in = jnp.sum(before * onehot, axis=1).astype(jnp.int32)
    position = target_dev * capacity + rank_in
    hit = position[None, :] == jnp.arange(devices * capacity, dtype=jnp.int32)[:, None]
    out_slots = slots_dev + jnp.sum(jnp.where(hit, target_slot[None, :] - slots_dev, 0), axis=1)
    outgoing = partials(position, source, regrid_weights, devices * capacity)
    axes = ("band", "tile")
    arrived = lax.all_to_all(
        outgoing.reshape(devices, capacity, fields, block_len), axes, 0, 0, tiled=True
    )
    arrived_slots = lax.all_to_all(
        out_slots.reshape(devices, capacity), axes, 0, 0, tiled=True
    )
    grid = collect(
        arrived_slots.reshape(-1), arrived.reshape(devices * capacity, fields, block_len), slots_dev
    )
    tiles = grid.reshape(faces, rows, fields, block_len)
    pick = jnp.eye(block_len, dtype=BF)[jnp.array([0, block_len - 1])]
    ends = jnp.einsum("ep,tcp->etc", pick, grid, preferred_element_type=F32).astype(BF)
    ends = ends.reshape(2, faces, rows, fields)
    halos = halos_of(
        tiles[:, 0].transpose(0, 2, 1),
        tiles[:, -1].transpose(0, 2, 1),
        ends[0],
        ends[1],
        seam_table,
    )
    hidden, ends = conv(True, grid, halos, conv1_weight, conv1_bias, faces, rows, block_len)
    tiles = hidden.reshape(faces, rows, block_len, hidden.shape[2])
    halos = halos_of(
        tiles[:, 0], tiles[:, -1], ends[0].astype(BF), ends[1].astype(BF), seam_table
    )
    return conv(False, hidden, halos, conv2_weight, conv2_bias, faces, rows, block_len)


def solution(mesh):
    return jax.shard_map(
        local,
        mesh=mesh,
        in_specs=(
            P(None, ("band", "tile")),
            P(("band", "tile"), None, None, None),
            P(("band", "tile"), None),
            P(("band", "tile"), None),
            P(),
            P(),
            P(),
            P(),
            P(),
        ),
        out_specs=P(None, None, "band", "tile"),
        check_vma=False,
    )
```

profile of v0, /device:TPU:5, one launch (start us, length us, event | category | flops | bytes accessed | tf_op | source)
XLA Modules:
  0.0 616.5 jit_solution(5980821920272036998)
XLA Ops:
  9.4 6.4 %all-to-all-start = ((s32[32,1,24]{2,1,0:T(1,128)}), s32[32,1,24]{2,1,0:T(1,128)S(1)}, u32[]{:S(2)}, u32[]{:S(2)}) async-start(s32[32,1,24]{2,1,0:T(1,128)} %bitcast), calls=%async_computation | async-start | bytes 32768 | tf_op jit(solution)/shard_map/all_to_all | solution.py:410
  15.8 16.2 %partials.1 = bf16[768,40,128]{2,1,0:T(8,128)(2,1)} custom-call(s32[256]{0:T(256)} %copy-done.6, bf16[40,8192]{1,0:T(8,128)(2,1)} %src_ref.1, bf16[64,4,128,128]{3,2,1,0:T(8,128)(2,1)} %w_ref.1), custom_call_target="tpu_custom_call" | custom-call | tf_op jit(solution)/shard_map/partials/pallas_call | solution.py:56
  32.1 5.9 all-to-all-start.1
  40.5 169.2 %all-to-all-done.1 = bf16[32,24,40,128]{3,2,1,0:T(8,128)(2,1)} async-done(((bf16[32,24,40,128]{3,2,1,0:T(8,128)(2,1)}), bf16[32,24,40,128]{3,2,1,0:T(8,128)(2,1)}, u32[]{:S(2)}, u32[]{:S(2)}) %all-to-all-start.1) | async-done | bytes 7864352 | tf_op jit(solution)/shard_map/all_to_all | solution.py:407
  209.6 13.8 %collect.1.x_ref = bf16[768,40,128]{2,1,0:T(8,128)(2,1)} custom-call(s32[768]{0:T(1024)} %reshape.782.slot_ref, bf16[768,40,128]{2,1,0:T(8,128)(2,1)} %bitcast.2.arr_ref), custom_call_target="tpu_custom_call" | custom-call | tf_op jit(solution)/shard_map/collect/pallas_call | solution.py:96
  223.4 5.4 fusion.4
  230.0 5.6 all-to-all-start.3
  238.0 6.6 %all-to-all-start.2 = ((bf16[8,192,40]{1,2,0:T(8,128)(2,1)}), bf16[8,192,40]{1,2,0:T(8,128)(2,1)S(1)}, u32[]{:S(2)}, u32[]{:S(2)}) async-start(bf16[8,192,40]{1,2,0:T(8,128)(2,1)} %copy.487), calls=%async_computation.2 | async-start | bytes 327680 | tf_op jit(solution)/shard_map/all_to_all | solution.py:301
  244.7 6.4 %all-to-all-done.2 = bf16[8,192,40]{1,2,0:T(8,128)(2,1)S(1)} async-done(((bf16[8,192,40]{1,2,0:T(8,128)(2,1)}), bf16[8,192,40]{1,2,0:T(8,128)(2,1)S(1)}, u32[]{:S(2)}, u32[]{:S(2)}) %all-to-all-start.2) | async-done | bytes 122912 | tf_op jit(solution)/shard_map/all_to_all | solution.py:301
  256.3 4.0 collective-permute-start
  260.3 3.4 collective-permute-done.1
  263.8 9.4 %collective-permute-done = bf16[12,128,40]{2,1,0:T(8,128)(2,1)S(1)} collective-permute-done((bf16[12,128,40]{2,1,0:T(8,128)(2,1)S(1)}, bf16[12,128,40]{2,1,0:T(8,128)(2,1)S(1)}, u32[]{:S(2)}, u32[]{:S(2)}) %collective-permute-start) | collective-permute-done | bytes 122912 | tf_op jit(solution)/shard_map/ppermute | solution.py:354
  279.4 32.7 %all-gather.5.cloned.1.call-done = bf16[24576,40]{0,1:T(8,128)(2,1)} async-done(((bf16[768,40]{0,1:T(8,128)(2,1)}), bf16[24576,40]{0,1:T(8,128)(2,1)}) %all-gather.5.cloned.1.call-update) | async-done | bytes 1966096 | tf_op jit(solution)/shard_map/all_gather | solution.py:304
  312.2 6.7 %reshape.787 = bf16[384,64,40]{1,0,2:T(8,128)(2,1)} reshape(bf16[24576,40]{0,1:T(8,128)(2,1)} %all-gather.5.cloned.1.call-done) | data formatting | bytes 3932160 | tf_op jit(solution)/shard_map/reshape | solution.py:305
  318.9 6.5 %copy.490 = bf16[384,64,40]{1,2,0:T(8,128)(2,1)} copy(bf16[384,64,40]{1,0,2:T(8,128)(2,1)} %reshape.787) | data formatting | bytes 3932160 | tf_op jit(solution)/shard_map/reshape | solution.py:305
  342.0 66.2 %conv1.1 = (bf16[768,128,128]{2,1,0:T(8,128)(2,1)}, f32[2,12,64,128]{3,2,1,0:T(8,128)}) custom-call(bf16[768,40,128]{2,1,0:T(8,128)(2,1)} %collect.1.x_ref, bf16[12,130,40]{2,1,0:T(8,128)(2,1)} %pad_maximum_fusion.top_ref, bf16[12,130,40]{2,1,0:T(8,128)(2,1)} %pad_maximum_fusion.1.bot_ref, f32[12,64,40]{2,1,0:T(8,128)} %slice_convert_fusion.5.left_ref, ...), custom_call_target="tpu_custom_call" | custom-call | tf_op jit(solution)/shard_map/conv1/pallas_call | solution.py:271
  410.1 4.1 all-to-all-start.5
  417.9 3.6 all-to-all-start.4
  421.7 11.0 %all-to-all-done.4 = bf16[8,192,128]{2,1,0:T(8,128)(2,1)S(1)} async-done(((bf16[8,192,128]{2,1,0:T(8,128)(2,1)}), bf16[8,192,128]{2,1,0:T(8,128)(2,1)S(1)}, u32[]{:S(2)}, u32[]{:S(2)}) %all-to-all-start.4) | async-done | bytes 393248 | tf_op jit(solution)/shard_map/all_to_all | solution.py:301
  440.4 14.4 %collective-permute-done.4 = bf16[12,128,128]{2,1,0:T(8,128)(2,1)S(1)} collective-permute-done((bf16[12,128,128]{2,1,0:T(8,128)(2,1)S(1)}, bf16[12,128,128]{2,1,0:T(8,128)(2,1)S(1)}, u32[]{:S(2)}, u32[]{:S(2)}) %collective-permute-start.4) | collective-permute-done | bytes 393248 | tf_op jit(solution)/shard_map/ppermute | solution.py:354
  455.5 4.8 collective-permute-start.7
  462.4 47.0 %all-gather.7.cloned.1.call-done = bf16[24576,128]{1,0:T(8,128)(2,1)} async-done(((bf16[768,128]{1,0:T(8,128)(2,1)}), bf16[24576,128]{1,0:T(8,128)(2,1)}) %all-gather.7.cloned.1.call-update) | async-done | bytes 6291472 | tf_op jit(solution)/shard_map/all_gather | solution.py:304
  509.4 4.0 gather_fusion.2
  519.6 90.1 %conv2.1 = bf16[128,12,64,128]{3,2,1,0:T(8,128)(2,1)} custom-call(bf16[768,128,128]{2,1,0:T(8,128)(2,1)} %get-tuple-element.7.x_ref, bf16[12,130,128]{2,1,0:T(8,128)(2,1)} %pad_maximum_fusion.2.top_ref, bf16[12,130,128]{2,1,0:T(8,128)(2,1)} %pad_maximum_fusion.3.bot_ref, f32[12,64,128]{2,1,0:T(8,128)} %slice_convert_fusion.3.left_ref, ...), custom_call_target="tpu_custom_call" | custom-call | tf_op jit(solution)/shard_map/conv2/pallas_call | solution.py:271
  (142 shorter events, 59.1 us)
Async XLA Ops:
  8.5 7.3 %copy-start.6 = (s32[256]{0:T(256)}, s32[256]{0:T(256)S(1)}, u32[]{:S(2)}) copy-start(s32[256]{0:T(256)S(1)} %convert_add_fusion.pos_ref) | copy-start | bytes 3076
  9.4 22.6 %all-to-all-start = ((s32[32,1,24]{2,1,0:T(1,128)}), s32[32,1,24]{2,1,0:T(1,128)S(1)}, u32[]{:S(2)}, u32[]{:S(2)}) async-start(s32[32,1,24]{2,1,0:T(1,128)} %bitcast), calls=%async_computation | async-start | bytes 32768 | tf_op jit(solution)/shard_map/all_to_all | solution.py:410
  32.1 177.6 %all-to-all-start.1 = ((bf16[32,24,40,128]{3,2,1,0:T(8,128)(2,1)}), bf16[32,24,40,128]{3,2,1,0:T(8,128)(2,1)}, u32[]{:S(2)}, u32[]{:S(2)}) async-start(bf16[32,24,40,128]{3,2,1,0:T(8,128)(2,1)} %bitcast.207), calls=%async_computation.1 | async-start | bytes 15728640 | tf_op jit(solution)/shard_map/all_to_all | solution.py:407
  228.8 23.0 %copy-start.4 = (s32[12,4,3]{0,1,2:T(4,128)S(1)}, s32[12,4,3]{0,1,2:T(4,128)}, u32[]{:S(2)}) copy-start(s32[12,4,3]{0,1,2:T(4,128)} %param.14) | copy-start | bytes 1732
  228.8 23.9 %copy-start.3 = (bf16[9,128,40]{1,2,0:T(8,128)(2,1)S(1)}, bf16[9,128,40]{1,2,0:T(8,128)(2,1)}, u32[]{:S(2)}) copy-start(bf16[9,128,40]{1,2,0:T(8,128)(2,1)} %param.15) | copy-start | bytes 276484
  228.8 25.3 %copy-start.8 = (f32[128]{0:T(128)S(1)}, f32[128]{0:T(128)}, u32[]{:S(2)}) copy-start(f32[128]{0:T(128)} %param.16) | copy-start | bytes 1540
  230.0 8.0 %all-to-all-start.3 = ((bf16[4,192,40]{1,2,0:T(8,128)(2,1)}), bf16[4,192,40]{1,2,0:T(8,128)(2,1)S(1)}, u32[]{:S(2)}, u32[]{:S(2)}) async-start(bf16[4,192,40]{1,2,0:T(8,128)(2,1)} %copy.489), calls=%async_computation.3 | async-start | bytes 163840 | tf_op jit(solution)/shard_map/all_to_all | solution.py:302
  238.0 13.0 %all-to-all-start.2 = ((bf16[8,192,40]{1,2,0:T(8,128)(2,1)}), bf16[8,192,40]{1,2,0:T(8,128)(2,1)S(1)}, u32[]{:S(2)}, u32[]{:S(2)}) async-start(bf16[8,192,40]{1,2,0:T(8,128)(2,1)} %copy.487), calls=%async_computation.2 | async-start | bytes 327680 | tf_op jit(solution)/shard_map/all_to_all | solution.py:301
  244.6 67.5 %all-gather.5.cloned.1.call-start = ((), (), s32[]{:S(2)}) async-start(), calls=%async_computation.6 | async-start | bytes 2027520 | tf_op jit(solution)/shard_map/all_gather | solution.py:304
  252.7 72.7 %copy-start.5 = (s32[1024]{0:T(1024)}, s32[1024]{0:T(1024)S(1)}, u32[]{:S(2)}) copy-start(s32[1024]{0:T(1024)S(1)} %pad_clamp_fusion) | copy-start | bytes 12292
  252.8 11.0 %collective-permute-start.1 = (bf16[12,128,40]{2,1,0:T(8,128)(2,1)S(1)}, bf16[12,128,40]{2,1,0:T(8,128)(2,1)S(1)}, u32[]{:S(2)}, u32[]{:S(2)}) collective-permute-start(bf16[12,128,40]{2,1,0:T(8,128)(2,1)S(1)} %bitcast.218), channel_id=1, source_target_pairs={{4,0},{8,4},{12,8},{16,12},{20,16},{24,20},{28,24},{5,1},{9,5},{13... | collective-permute-start | bytes 368648 | tf_op jit(solution)/shard_map/ppermute | solution.py:354
  256.3 16.8 %collective-permute-start = (bf16[12,128,40]{2,1,0:T(8,128)(2,1)S(1)}, bf16[12,128,40]{2,1,0:T(8,128)(2,1)S(1)}, u32[]{:S(2)}, u32[]{:S(2)}) collective-permute-start(bf16[12,128,40]{2,1,0:T(8,128)(2,1)S(1)} %bitcast.217), channel_id=1, source_target_pairs={{0,4},{4,8},{8,12},{12,16},{16,20},{20,24},{24,28},{1,5},{5,9},{9,... | collective-permute-start | bytes 368648 | tf_op jit(solution)/shard_map/ppermute | solution.py:354
  273.2 45.7 %copy-start = (bf16[12,128,40]{2,1,0:T(8,128)(2,1)}, bf16[12,128,40]{2,1,0:T(8,128)(2,1)S(1)}, u32[]{:S(2)}) copy-start(bf16[12,128,40]{2,1,0:T(8,128)(2,1)S(1)} %collective-permute-done) | copy-start | bytes 368644
  274.0 64.9 %collective-permute-start.3 = (bf16[12,66,40]{2,1,0:T(8,128)(2,1)}, bf16[12,66,40]{2,1,0:T(8,128)(2,1)}, u32[]{:S(2)}, u32[]{:S(2)}) collective-permute-start(bf16[12,66,40]{2,1,0:T(8,128)(2,1)} %pad_maximum_fusion.5), channel_id=1, source_target_pairs={{1,0},{2,1},{3,2},{5,4},{6,5},{7,6},{9,8},{10,9},{11,10},{13,12},{... | collective-permute-start | bytes 190088 | tf_op jit(solution)/shard_map/ppermute | solution.py:354
  278.0 58.6 %collective-permute-start.2 = (bf16[12,66,40]{2,1,0:T(8,128)(2,1)}, bf16[12,66,40]{2,1,0:T(8,128)(2,1)}, u32[]{:S(2)}, u32[]{:S(2)}) collective-permute-start(bf16[12,66,40]{2,1,0:T(8,128)(2,1)} %pad_maximum_fusion.4), channel_id=1, source_target_pairs={{0,1},{1,2},{2,3},{4,5},{5,6},{6,7},{8,9},{9,10},{10,11},{12,13},{... | collective-permute-start | bytes 190088 | tf_op jit(solution)/shard_map/ppermute | solution.py:354
  337.7 3.4 copy-start.1
  408.2 29.6 %copy-start.2 = (bf16[9,128,128]{2,1,0:T(8,128)(2,1)S(1)}, bf16[9,128,128]{2,1,0:T(8,128)(2,1)}, u32[]{:S(2)}) copy-start(bf16[9,128,128]{2,1,0:T(8,128)(2,1)} %param.17) | copy-start | bytes 884740
  410.1 7.8 %all-to-all-start.5 = ((bf16[4,192,128]{2,1,0:T(8,128)(2,1)}), bf16[4,192,128]{2,1,0:T(8,128)(2,1)S(1)}, u32[]{:S(2)}, u32[]{:S(2)}) async-start(bf16[4,192,128]{2,1,0:T(8,128)(2,1)} %bitcast.68), calls=%async_computation.5 | async-start | bytes 393216 | tf_op jit(solution)/shard_map/all_to_all | solution.py:302
  417.9 14.7 %all-to-all-start.4 = ((bf16[8,192,128]{2,1,0:T(8,128)(2,1)}), bf16[8,192,128]{2,1,0:T(8,128)(2,1)S(1)}, u32[]{:S(2)}, u32[]{:S(2)}) async-start(bf16[8,192,128]{2,1,0:T(8,128)(2,1)} %bitcast.65), calls=%async_computation.4 | async-start | bytes 786432 | tf_op jit(solution)/shard_map/all_to_all | solution.py:301
  421.6 87.8 %all-gather.7.cloned.1.call-start = ((), (), s32[]{:S(2)}) async-start(), calls=%async_computation.7 | async-start | bytes 6488064 | tf_op jit(solution)/shard_map/all_gather | solution.py:304
  434.6 20.1 %collective-permute-start.4 = (bf16[12,128,128]{2,1,0:T(8,128)(2,1)S(1)}, bf16[12,128,128]{2,1,0:T(8,128)(2,1)S(1)}, u32[]{:S(2)}, u32[]{:S(2)}) collective-permute-start(bf16[12,128,128]{2,1,0:T(8,128)(2,1)S(1)} %get-tuple-element.17), channel_id=1, source_target_pairs={{0,4},{4,8},{8,12},{12,16},{16,20},{20,24},{24,28},{1,5},{5,9},{9,... | collective-permute-start | bytes 1179656 | tf_op jit(solution)/shard_map/ppermute | solution.py:354
  438.1 16.7 %collective-permute-start.5 = (bf16[12,128,128]{2,1,0:T(8,128)(2,1)S(1)}, bf16[12,128,128]{2,1,0:T(8,128)(2,1)S(1)}, u32[]{:S(2)}, u32[]{:S(2)}) collective-permute-start(bf16[12,128,128]{2,1,0:T(8,128)(2,1)S(1)} %get-tuple-element.18), channel_id=1, source_target_pairs={{4,0},{8,4},{12,8},{16,12},{20,16},{24,20},{28,24},{5,1},{9,5},{13... | collective-permute-start | bytes 1179656 | tf_op jit(solution)/shard_map/ppermute | solution.py:354
  455.5 59.5 %collective-permute-start.7 = (bf16[12,66,128]{2,1,0:T(8,128)(2,1)}, bf16[12,66,128]{2,1,0:T(8,128)(2,1)}, u32[]{:S(2)}, u32[]{:S(2)}) collective-permute-start(bf16[12,66,128]{2,1,0:T(8,128)(2,1)} %pad_maximum_fusion.7), channel_id=1, source_target_pairs={{1,0},{2,1},{3,2},{5,4},{6,5},{7,6},{9,8},{10,9},{11,10},{13,12},{... | collective-permute-start | bytes 608264 | tf_op jit(solution)/shard_map/ppermute | solution.py:354
  461.1 54.8 %collective-permute-start.6 = (bf16[12,66,128]{2,1,0:T(8,128)(2,1)}, bf16[12,66,128]{2,1,0:T(8,128)(2,1)}, u32[]{:S(2)}, u32[]{:S(2)}) collective-permute-start(bf16[12,66,128]{2,1,0:T(8,128)(2,1)} %pad_maximum_fusion.6), channel_id=1, source_target_pairs={{0,1},{1,2},{2,3},{4,5},{5,6},{6,7},{8,9},{9,10},{10,11},{12,13},{... | collective-permute-start | bytes 608264 | tf_op jit(solution)/shard_map/ppermute | solution.py:354
  (1 other events, 2.2 us)
Sparse Core Ops, SparseCore 0:
  251.9 60.2 all-gather.4
  433.5 75.7 all-gather.6
where the time goes:
time: 620 us; the launch traced here: 617 us
  waiting for transfers between devices  295 us (48%)
  Pallas kernels  186 us (30%)
  starting transfers between devices  52.9 us (9%)
  local copies, waits for them, and re-layouts  36.3 us (6%)
  other arithmetic  23.2 us (4%)
  between operations  14 us (2%)
  matrix products  8.59 us (1%)
    all_to_all x1, waiting for transfers between devices, local(): lax.all_to_all(outgoing.reshape(devices, capacity, fields, block_len), ax...  169 us
    pallas_call x2, Pallas kernels, conv(): pl.pallas_call(functools.partial(conv_kernel, first), out_shape=out_shape...  156 us
    all_gather x2, waiting for transfers between devices, halos_of(): every = lax.all_gather(mine, ('band', 'tile'), axis=0, tiled=False)  79.7 us
    ppermute x8, waiting for transfers between devices, shift(): return lax.ppermute(x, axis, pairs)  27.2 us
    ppermute x8, starting transfers between devices, shift(): return lax.ppermute(x, axis, pairs)  20.6 us
    all_to_all x2, waiting for transfers between devices, halos_of(): row_part = lax.all_to_all(row_edge, 'band', 0, 0, tiled=True)  17.4 us
    pallas_call x1, Pallas kernels, partials(): pl.pallas_call(partial_kernel, out_shape=jax.ShapeDtypeStruct((slots, fie...  16.2 us
    pallas_call x1, Pallas kernels, collect(): pl.pallas_call(collect_kernel, out_shape=jax.ShapeDtypeStruct((slots_dev,...  13.8 us
  transfers between devices with their start and end apart: 16, of which 9 were waited for; matrix products, arithmetic and copies ran while one was open for 8% of the time, Pallas kernels for 3%

commit v1 on v0

--- a/solution.py
+++ b/solution.py
@@ -12,6 +12,8 @@
 VMEM_LIMIT = 60 * 1024 * 1024
 PAIRS = 8
 UNROLLED = True
+CH = 16
+MESH = pl.DeviceIdType.MESH
 GELU_COEF = (
     0.7978842684146765,
     0.03633414911622174,
@@ -112,13 +114,16 @@
     first, x_ref, top_ref, bot_ref, left_ref, right_ref, wa_ref, wb_ref, b_ref, out_ref, *scratch
 ):
     if first:
-        ends, scratch = scratch[0], scratch[1:]
-    sl, win = scratch[0], scratch[1]
+        ends_ref, ends = scratch[0], scratch[-1]
+        scratch = scratch[1:]
+    sl, win, side = scratch[0], scratch[1], scratch[2]
     rows = out_ref.shape[0] if first else out_ref.shape[2]
     cols = sl.shape[1]
     width = sl.shape[2] // 2
-    chan = left_ref.shape[-1]
+    chan = x_ref.shape[1]
     slots = win.shape[0]
+    side[0] = left_ref[0, CH : CH + rows, :].astype(F32)
+    side[1] = right_ref[0, CH : CH + rows, :].astype(F32)
 
     def put(slot, pair, parity, row32, lo, hi):
         win[slot, 8 : 8 + cols, :] = row32
@@ -135,11 +140,6 @@
             sl[pair, :, base + cols : base + 2 * cols] = row32.astype(BF)
             sl[pair, :, base + 2 * cols : base + 3 * cols] = after.astype(BF)
 
-    def wide(v):
-        if first:
-            v = jnp.concatenate([v, jnp.zeros((v.shape[0], cols - chan), v.dtype)], axis=1)
-        return v
-
     def row_at(r):
         if first:
             y = x_ref[r].astype(F32)
@@ -148,8 +148,8 @@
         return x_ref[r].astype(F32)
 
     def halo_row(ref):
-        full = wide(ref[0].astype(F32))
-        return full[:cols], full[cols : cols + 1], full[cols + 1 : cols + 2]
+        full = ref[0].astype(F32)
+        return full[CH : CH + cols], full[CH - 1 : CH], full[CH + cols : CH + cols + 1]
 
     def put_row(r, k):
         put(
@@ -157,8 +157,8 @@
             r // 2 + k % 2 if isinstance(r, int) else (r - k % 2) // 2 + k % 2,
             1 - k % 2,
             row_at(r),
-            wide(left_ref[0, pl.ds(r, 1), :]),
-            wide(right_ref[0, pl.ds(r, 1), :]),
+            side[0, pl.ds(r, 1), :],
+            side[1, pl.ds(r, 1), :],
         )
 
     row, lo, hi = halo_row(top_ref)
@@ -190,10 +190,10 @@
                     part = y[p * cols : (p + 1) * cols, q * hid : (q + 1) * hid].astype(BF)
                     r = 2 * (p0 + p) + q
                     out_ref[r] = part
-                    ends[0, 0, pl.ds(r, 1), :] = part[:1].astype(F32)
-                    ends[1, 0, pl.ds(r, 1), :] = part[cols - 1 :].astype(F32)
+                    ends[0, pl.ds(r, 1), :] = part[:1].astype(F32)
+                    ends[1, pl.ds(r, 1), :] = part[cols - 1 :].astype(F32)
             return
-        flip = scratch[2].at[g % 2 if unroll else 0]
+        flip = scratch[3].at[g % 2 if unroll else 0]
         for p in range(PAIRS):
             for q in range(2):
                 part = y[p * cols : (p + 1) * cols, q * hid : (q + 1) * hid]
@@ -227,6 +227,8 @@
             return 0
 
         lax.fori_loop(0, rows // n, chunk, 0)
+    if first:
+        ends_ref[:, 0] = ends[...].astype(BF)
 
 
 def conv(first, x, halos, weight, bias, face_count, rows, out_cols):
@@ -250,18 +252,20 @@
     scratch = [
         pltpu.VMEM((rows // 2 + 1, cols, 2 * width), BF),
         pltpu.VMEM((8, cols + 16, cols), F32),
+        pltpu.VMEM((2, rows, cols), F32),
     ]
     if first:
         bias_in = jnp.concatenate([bias, bias])[None, :]
         bias_spec = pl.BlockSpec((1, 2 * hid), lambda f: (0, 0))
         out_shape = (
             jax.ShapeDtypeStruct((face_count * rows, cols, hid), BF),
-            jax.ShapeDtypeStruct((2, face_count, rows, hid), F32),
+            jax.ShapeDtypeStruct((2, face_count, rows, hid), BF),
         )
         out_spec = (
             pl.BlockSpec((rows, cols, hid), lambda f: (f, 0, 0)),
             pl.BlockSpec((2, 1, rows, hid), lambda f: (0, f, 0, 0)),
         )
+        scratch.append(pltpu.VMEM((2, rows, hid), F32))
     else:
         bias_in = bias
         bias_spec = pl.BlockSpec(memory_space=pltpu.SMEM)
@@ -289,88 +293,167 @@
     )(x, top, bot, left, right, wa, wb, bias_in)
 
 
-def halos_of(top, bottom, left, right, seam_table):
-    faces, cols, chan = top.shape
-    rows = left.shape[1]
+def halo_kernel(line_refs, nb, nt, tab_ref, *refs):
+    ins, refs = refs[:line_refs], refs[line_refs:]
+    tops, bots, lefts, rights, cand, pick, recv, send, met = refs
+    faces, rows, cols = tops.shape[0], lefts.shape[1] - 2 * CH, tops.shape[1] - 2 * CH
+    if line_refs == 2:
+        top, bot = ins[0].at[:, 0], ins[0].at[:, rows - 1]
+        left, right = ins[1].at[0], ins[1].at[1]
+    else:
+        top, bot, left, right = ins
+    b, t = lax.axis_index("band"), lax.axis_index("tile")
+    me = b * nt + t
+    per_col, per_row = rows // CH, cols // CH
+    chunks = nt * per_row
+    classes = chunks // 2
+    step = nb * nt // classes
+    both = jnp.logical_and
+    last_b, last_t = b == nb - 1, t == nt - 1
+    TOP, BOT, LEFT, RIGHT = 0, 3, 6, 9
+    main, lead = pl.ds(CH, cols), pl.ds(0, CH)
+    main_v, trail_v = pl.ds(CH, rows), pl.ds(CH + rows, CH)
+    trail = pl.ds(CH + cols, CH)
+    started = []
+
+    def go(cond, src, dst, sem, db, dt, own=True):
+        same = db * nt + dt == me
+        copy = pltpu.make_async_remote_copy(
+            src_ref=src, dst_ref=dst, send_sem=send.at[len(started)], recv_sem=sem,
+            device_id=(db, dt), device_id_type=MESH,
+        )
+        away = both(cond, jnp.logical_not(same)) if own else cond
+        pl.when(away)(copy.start)
+        if own:
+            pl.when(both(cond, same))(pltpu.make_async_copy(src, dst, sem).start)
+        started.append((away, copy))
+
+    def taken(cond, ref, sem):
+        pl.when(cond)(pltpu.make_async_copy(ref, ref, sem).wait)
+
+    lines = [
+        (b == 0, top, t * per_row, per_row),
+        (last_b, bot, t * per_row, per_row),
+        (t == 0, left, b * per_col, per_col),
+        (last_t, right, b * per_col, per_col),
+    ]
+    for side, (cond, line, first, count) in enumerate(lines):
+        for i in range(count):
+            k = first + i
+            upper = k // classes
+            at = (k + upper * (chunks - 1 - 2 * k)) * step
+            go(cond, line.at[:, pl.ds(i * CH, CH)], cand.at[upper, side], met, at // nt, at % nt)
+    for cond, line, dst, base, db in (
+        (b > 0, top, bots, BOT, b - 1),
+        (b < nb - 1, bot, tops, TOP, b + 1),
+    ):
+        go(cond, line, dst.at[:, main], recv.at[base], db, t, False)
+        go(both(cond, t > 0), line.at[:, pl.ds(0, CH)], dst.at[:, trail], recv.at[base + 2],
+           db, t - 1, False)
+        go(both(cond, t < nt - 1), line.at[:, pl.ds(cols - CH, CH)], dst.at[:, lead],
+           recv.at[base + 1], db, t + 1, False)
+    go(t > 0, left, rights.at[:, main_v], recv.at[RIGHT], b, t - 1, False)
+    go(t < nt - 1, right, lefts.at[:, main_v], recv.at[LEFT], b, t + 1, False)
+
+    meets = both(me % step == 0, me // step < classes)
+    taken(meets, cand, met)
+    near = lax.broadcasted_iota(jnp.int32, (CH, CH), 0)
+    far = lax.broadcasted_iota(jnp.int32, (CH, CH), 1)
+    mirror = jnp.where(near + far == CH - 1, 1.0, 0.0).astype(BF)
+
+    @pl.when(meets)
+    def _():
+        def choose(f, _):
+            for side in range(4):
+                e = (f * 4 + side) * 3
+                face, edge, rev = tab_ref[e], tab_ref[e + 1], tab_ref[e + 2]
+                for h in range(2):
+                    turned = jnp.dot(mirror, cand[1 - h, edge, face], preferred_element_type=F32)
+                    pick[h, side, f] = jnp.where(
+                        rev == 1, turned, cand[h, edge, face].astype(F32)
+                    ).astype(BF)
+            return 0
+
+        lax.fori_loop(0, faces, choose, 0)
+
+    low = me // step
+    for h in range(2):
+        k = low if h == 0 else chunks - 1 - low
+        for side in range(4):
+            src = pick.at[h, side]
+            if side < 2:
+                owner, off = k // per_row, k % per_row
+                dst, base, db = ((tops, TOP, 0), (bots, BOT, nb - 1))[side]
+                size, per, ends, length = nt, per_row, (lead, trail), cols
+                dev = lambda o: (db, o)
+            else:
+                owner, off = k // per_col, k % per_col
+                dst, base, dt = ((lefts, LEFT, 0), (rights, RIGHT, nt - 1))[side - 2]
+                size, per, ends, length = nb, per_col, (lead, trail_v), rows
+                dev = lambda o: (o, dt)
+            go(meets, src, dst.at[:, pl.ds(CH + off * CH, CH)], recv.at[base], *dev(owner))
+            go(both(meets, both(off == per - 1, owner < size - 1)), src, dst.at[:, ends[0]],
+               recv.at[base + 1], *dev(owner + 1))
+            go(both(meets, both(off == 0, owner > 0)), src, dst.at[:, ends[1]],
+               recv.at[base + 2], *dev(owner - 1))
+
+    for dst, base in ((tops, TOP), (bots, BOT)):
+        taken(me >= 0, dst.at[:, main], recv.at[base])
+        taken(t > 0, dst.at[:, lead], recv.at[base + 1])
+        taken(t < nt - 1, dst.at[:, trail], recv.at[base + 2])
+    for dst, base, cond in ((lefts, LEFT, t == 0), (rights, RIGHT, last_t)):
+        taken(me >= 0, dst.at[:, main_v], recv.at[base])
+        taken(both(cond, b > 0), dst.at[:, lead], recv.at[base + 1])
+        taken(both(cond, b < nb - 1), dst.at[:, trail_v], recv.at[base + 2])
+
+    for cond, src, end in ((t == 0, lefts, lead), (last_t, rights, trail)):
+        for present, dst, part, row in (
+            (b > 0, tops, lead, CH - 1),
+            (b < nb - 1, bots, trail_v, 0),
+        ):
+            turn = ((CH - 1 if end is lead else 0) - row) % CH
+
+            @pl.when(both(cond, present))
+            def _():
+                def corner(f, _):
+                    v = src[f, part, :].astype(F32)
+                    dst[f, end, :] = (pltpu.roll(v, turn, 0) if turn else v).astype(BF)
+                    return 0
+
+                lax.fori_loop(0, faces, corner, 0)
+
+            @pl.when(both(cond, jnp.logical_not(present)))
+            def _():
+                dst[:, end, :] = jnp.zeros((faces, CH, dst.shape[2]), BF)
+
+    for away, copy in started:
+        pl.when(away)(copy.wait_send)
+
+
+def halo_exchange(lines, seam_table, rows, cols, name):
     nb, nt = lax.axis_size("band"), lax.axis_size("tile")
-    band, tile = lax.axis_index("band"), lax.axis_index("tile")
-    side = cols * nt
-
-    row_edge = jnp.where(band == 0, top, bottom).reshape(nb, faces * cols // nb, chan)
-    col_edge = jnp.where(tile == 0, left, right).reshape(nt, faces * rows // nt, chan)
-    row_part = lax.all_to_all(row_edge, "band", 0, 0, tiled=True)
-    col_part = lax.all_to_all(col_edge, "tile", 0, 0, tiled=True)
-    mine = jnp.concatenate([row_part[0], row_part[-1], col_part[0], col_part[-1]], axis=0)
-    every = lax.all_gather(mine, ("band", "tile"), axis=0, tiled=False)
-    pieces = every.reshape(-1, rows, chan)
-    per_row, per_col = row_edge.shape[1] // rows, col_edge.shape[1] // rows
-    per_dev = 2 * (per_row + per_col)
-    per_tile = cols // rows
-    last_piece = side // rows - 1
-
-    def wanted(which, first, count):
-        at = first - 1 + jnp.arange(count + 2, dtype=jnp.int32)
-        face = seam_table[:, which, 0][:, None]
-        edge = seam_table[:, which, 1][:, None]
-        rev = seam_table[:, which, 2][:, None] == 1
-        q = jnp.clip(jnp.where(rev, last_piece - at, at), 0, last_piece)
-        c = face * per_tile + q % per_tile
-        on_row = (c // per_row * nt + q // per_tile) * per_dev + edge * per_row + c % per_row
-        on_col = (
-            (q * nt + face // per_col) * per_dev
-            + 2 * per_row
-            + (edge - 2) * per_col
-            + face % per_col
-        )
-        return jnp.where(edge < 2, on_row, on_col), jnp.broadcast_to(rev, q.shape)
-
-    asked = [
-        (0, tile * per_tile, per_tile),
-        (1, tile * per_tile, per_tile),
-        (2, band, 1),
-        (3, band, 1),
-    ]
-    parts = [wanted(*a) for a in asked]
-    index = jnp.concatenate([p[0] for p in parts], axis=1)
-    rev = jnp.concatenate([p[1] for p in parts], axis=1)
-    got = jnp.take(pieces, index.reshape(-1), axis=0, mode="clip")
-    flip = jnp.eye(rows, dtype=BF)[::-1]
-    flipped = jnp.einsum("pq,kqc->kpc", flip, got, preferred_element_type=F32).astype(BF)
-    got = jnp.where(rev.reshape(-1)[:, None, None], flipped, got)
-    got = got.reshape(faces, index.shape[1], rows, chan)
-    offset = [0]
-    for a in asked:
-        offset.append(offset[-1] + a[2] + 2)
-
-    def segments(which):
-        o, n, first = offset[which], asked[which][2], asked[which][1]
-        middle = got[:, o + 1 : o + 1 + n].reshape(faces, n * rows, chan)
-        lead = jnp.where(first > 0, got[:, o, -1:], 0)
-        trail = jnp.where(first + n <= last_piece, got[:, o + 1 + n, :1], 0)
-        return lead, middle, trail
-
-    def shift(x, axis, size, forward):
-        pairs = [(i, i + 1) if forward else (i + 1, i) for i in range(size - 1)]
-        return lax.ppermute(x, axis, pairs)
-
-    above = shift(bottom, "band", nb, True)
-    below = shift(top, "band", nb, False)
-    ext_left = jnp.concatenate([above[:, :1], left, below[:, :1]], axis=1)
-    ext_right = jnp.concatenate([above[:, -1:], right, below[:, -1:]], axis=1)
-    from_left = shift(ext_right, "tile", nt, True)
-    from_right = shift(ext_left, "tile", nt, False)
-    lefts = jnp.where(tile == 0, jnp.concatenate(segments(2), axis=1), from_left)
-    rights = jnp.where(tile == nt - 1, jnp.concatenate(segments(3), axis=1), from_right)
-
-    def line(at_edge, which, inner, at):
-        lead, middle, trail = segments(which)
-        lead = jnp.where(at_edge, lead, lefts[:, at : at + 1])
-        trail = jnp.where(at_edge, trail, rights[:, at : at + 1])
-        return jnp.concatenate([jnp.where(at_edge, middle, inner), lead, trail], axis=1)
-
-    tops = line(band == 0, 0, above, 0)
-    bots = line(band == nb - 1, 1, below, rows + 1)
-    return tops, bots, lefts[:, 1:-1].astype(F32), rights[:, 1:-1].astype(F32)
+    faces, chan = seam_table.shape[0], lines[0].shape[-1]
+    per_col, per_row = rows // CH, cols // CH
+    sends = 2 * per_col + 2 * per_row + 8 + 24
+    row_line = jax.ShapeDtypeStruct((faces, cols + 2 * CH, chan), BF)
+    col_line = jax.ShapeDtypeStruct((faces, rows + 2 * CH, chan), BF)
+    vmem = pl.BlockSpec(memory_space=pltpu.VMEM)
+    return pl.pallas_call(
+        functools.partial(halo_kernel, len(lines), nb, nt),
+        out_shape=(row_line, row_line, col_line, col_line),
+        in_specs=[pl.BlockSpec(memory_space=pltpu.SMEM)]
+        + [pl.BlockSpec(memory_space=pl.ANY)] * len(lines),
+        out_specs=(vmem,) * 4,
+        scratch_shapes=[
+            pltpu.VMEM((2, 4, faces, CH, chan), BF),
+            pltpu.VMEM((2, 4, faces, CH, chan), BF),
+            pltpu.SemaphoreType.DMA((12,)),
+            pltpu.SemaphoreType.DMA((sends,)),
+            pltpu.SemaphoreType.DMA,
+        ],
+        compiler_params=pltpu.CompilerParams(has_side_effects=True),
+        name=name,
+    )(seam_table.reshape(-1), *lines)
 
 
 def local(
@@ -417,18 +500,17 @@
     pick = jnp.eye(block_len, dtype=BF)[jnp.array([0, block_len - 1])]
     ends = jnp.einsum("ep,tcp->etc", pick, grid, preferred_element_type=F32).astype(BF)
     ends = ends.reshape(2, faces, rows, fields)
-    halos = halos_of(
-        tiles[:, 0].transpose(0, 2, 1),
-        tiles[:, -1].transpose(0, 2, 1),
-        ends[0],
-        ends[1],
-        seam_table,
-    )
+    spare = ((0, 0), (0, 0), (0, block_len - fields))
+    lines = [
+        jnp.pad(tiles[:, 0].transpose(0, 2, 1), spare),
+        jnp.pad(tiles[:, -1].transpose(0, 2, 1), spare),
+        jnp.pad(ends[0], spare),
+        jnp.pad(ends[1], spare),
+    ]
+    halos = halo_exchange(lines, seam_table, rows, block_len, "halo1")
     hidden, ends = conv(True, grid, halos, conv1_weight, conv1_bias, faces, rows, block_len)
     tiles = hidden.reshape(faces, rows, block_len, hidden.shape[2])
-    halos = halos_of(
-        tiles[:, 0], tiles[:, -1], ends[0].astype(BF), ends[1].astype(BF), seam_table
-    )
+    halos = halo_exchange([tiles, ends], seam_table, rows, block_len, "halo2")
     return conv(False, hidden, halos, conv2_weight, conv2_bias, faces, rows, block_len)
 
 

time: 620 us -> 462 us (0.75)
  waiting for transfers between devices: 295 us -> 166 us
  Pallas kernels: 186 us -> 264 us
  starting transfers between devices: 52.9 us -> 12.3 us
  local copies, waits for them, and re-layouts: 36.3 us -> 9.85 us
  other arithmetic: 23.2 us -> 3.85 us
  between operations: 14 us -> 0.18 us
    all_gather x2 -> x0, waiting for transfers between devices: 79.7 us -> none  [halos_of(): every = lax.all_gather(mine, ('band', 'tile'), axis=0, tiled=False)]
    pallas_call x0 -> x2, Pallas kernels: none -> 77.7 us  [halo_exchange(): pl.pallas_call(functools.partial(halo_kernel, len(lines), nb, nt), out_sh...]
    ppermute x8 -> x0, waiting for transfers between devices: 27.2 us -> none  [shift(): return lax.ppermute(x, axis, pairs)]
    ppermute x8 -> x0, starting transfers between devices: 20.6 us -> none  [shift(): return lax.ppermute(x, axis, pairs)]
    all_to_all x4 -> x0, starting transfers between devices: 20 us -> none  [the longest x2 10.3 us: halos_of(): row_part = lax.all_to_all(row_edge, 'band', 0, 0, tiled=True)]
    all_to_all x4 -> x0, waiting for transfers between devices: 19.2 us -> none  [the longest x2 17.4 us: halos_of(): row_part = lax.all_to_all(row_edge, 'band', 0, 0, tiled=True)]
    reshape x4 -> x1, local copies, waits for them, and re-layouts: 14.1 us -> 0.71 us  [halo_exchange(): seam_table.reshape(-1)]
    gather x3 -> x0, local copies, waits for them, and re-layouts: 9.28 us -> none  [halos_of(): got = jnp.take(pieces, index.reshape(-1), axis=0, mode='clip')]
  transfers between devices with their start and end apart: 16 -> 2, of which waited for: 9 -> 1; matrix products, arithmetic and copies ran while one was open for 8% -> 1% of each run, Pallas kernels for 3% -> 4%
where the time goes in v1:
time: 462 us; the launch traced here: 461 us
  Pallas kernels  264 us (57%)
  waiting for transfers between devices  166 us (36%)
  starting transfers between devices  12.3 us (3%)
  local copies, waits for them, and re-layouts  9.85 us (2%)
  matrix products  5.59 us (1%)
    all_to_all x1, waiting for transfers between devices, local(): lax.all_to_all(outgoing.reshape(devices, capacity, fields, block_len), ax...  166 us
    pallas_call x2, Pallas kernels, conv(): pl.pallas_call(functools.partial(conv_kernel, first), out_shape=out_shape...  156 us
    pallas_call x2, Pallas kernels, halo_exchange(): pl.pallas_call(functools.partial(halo_kernel, len(lines), nb, nt), out_sh...  77.7 us
    pallas_call x1, Pallas kernels, partials(): pl.pallas_call(partial_kernel, out_shape=jax.ShapeDtypeStruct((slots, fie...  16.2 us
    pallas_call x1, Pallas kernels, collect(): pl.pallas_call(collect_kernel, out_shape=jax.ShapeDtypeStruct((slots_dev,...  13.3 us
  transfers between devices with their start and end apart: 2, of which 1 were waited for; matrix products, arithmetic and copies ran while one was open for 1% of the time, Pallas kernels for 4%

profile of v1, /device:TPU:5, one launch (start us, length us, event | category | flops | bytes accessed | tf_op | source)
XLA Modules:
  0.0 461.2 jit_solution(2929561622523838624)
XLA Ops:
  0.0 0.7 broadcast_add_fusion.1
  0.9 0.8 copy.34
  2.2 0.7 add.51
  2.9 6.4 %all-to-all-start = ((s32[32,1,24]{2,1,0:T(1,128)}), s32[32,1,24]{2,1,0:T(1,128)S(1)}, u32[]{:S(2)}, u32[]{:S(2)}) async-start(s32[32,1,24]{2,1,0:T(1,128)} %bitcast), calls=%async_computation | async-start | bytes 32768 | tf_op jit(solution)/shard_map/all_to_all | solution.py:493
  9.3 16.2 %partials.1 = bf16[768,40,128]{2,1,0:T(8,128)(2,1)} custom-call(s32[256]{0:T(256)} %copy-done.2, bf16[40,8192]{1,0:T(8,128)(2,1)} %src_ref.1, bf16[64,4,128,128]{3,2,1,0:T(8,128)(2,1)} %w_ref.1), custom_call_target="tpu_custom_call" | custom-call | tf_op jit(solution)/shard_map/partials/pallas_call | solution.py:58
  25.6 5.9 %all-to-all-start.1 = ((bf16[32,24,40,128]{3,2,1,0:T(8,128)(2,1)}), bf16[32,24,40,128]{3,2,1,0:T(8,128)(2,1)}, u32[]{:S(2)}, u32[]{:S(2)}) async-start(bf16[32,24,40,128]{3,2,1,0:T(8,128)(2,1)} %bitcast.35), calls=%async_computation.1 | async-start | bytes 15728640 | tf_op jit(solution)/shard_map/all_to_all | solution.py:490
  31.6 0.7 reshape.83.tab_ref
  33.1 0.6 pad_maximum_fusion
  33.7 0.7 fusion.12
  34.5 0.9 fusion.8
  36.0 0.7 reduce.3
  36.7 0.7 reshape.80.slot_ref
  37.4 165.8 %all-to-all-done.1 = bf16[32,24,40,128]{3,2,1,0:T(8,128)(2,1)} async-done(((bf16[32,24,40,128]{3,2,1,0:T(8,128)(2,1)}), bf16[32,24,40,128]{3,2,1,0:T(8,128)(2,1)}, u32[]{:S(2)}, u32[]{:S(2)}) %all-to-all-start.1) | async-done | bytes 7864352 | tf_op jit(solution)/shard_map/all_to_all | solution.py:490
  203.1 13.3 %collect.1.x_ref = bf16[768,40,128]{2,1,0:T(8,128)(2,1)} custom-call(s32[768]{0:T(1024)} %reshape.80.slot_ref, bf16[768,40,128]{2,1,0:T(8,128)(2,1)} %bitcast.2.arr_ref), custom_call_target="tpu_custom_call" | custom-call | tf_op jit(solution)/shard_map/collect/pallas_call | solution.py:98
  216.4 5.4 %fusion.2 = bf16[2,768,40]{1,0,2:T(2,128)(2,1)S(1)} fusion(bf16[768,40,128]{2,1,0:T(8,128)(2,1)} %collect.1.x_ref, pred[2,128]{1,0:T(4,128)(4,1)S(1)} %gather_fusion), kind=kOutput, calls=%fused_computation.3 | convolution fusion | flops 15790080 | bytes 7987456 | tf_op jit(solution)/shard_map/ep,tcp->etc/dot_general | solution.py:501
  222.4 0.8 pad.25.refs_3_
  223.1 0.7 pad.24.refs_2_
  223.8 1.0 fusion.19
  225.1 0.8 pad.23.refs_1_
  226.2 0.8 pad.22.refs_0_
  227.0 42.8 %halo1.1 = (bf16[12,160,128]{2,1,0:T(8,128)(2,1)}, bf16[12,160,128]{2,1,0:T(8,128)(2,1)}, bf16[12,96,128]{2,1,0:T(8,128)(2,1)}, bf16[12,96,128]{2,1,0:T(8,128)(2,1)}) custom-call(s32[144]{0:T(256)} %reshape.83.tab_ref, bf16[12,128,128]{2,1,0:T(8,128)(2,1)} %pad.22.refs_0_, bf16[12,128,128]{2,1,0:T(8,128)(2,1)} %pad.23.refs_1_, ...), custom_call_target="tpu_custom_call" | custom-call | tf_op jit(solution)/shard_map/halo1/pallas_call | solution.py:441
  269.8 66.3 %conv1.1 = (bf16[768,128,128]{2,1,0:T(8,128)(2,1)}, bf16[2,12,64,128]{3,2,1,0:T(8,128)(2,1)}) custom-call(bf16[768,40,128]{2,1,0:T(8,128)(2,1)} %collect.1.x_ref, bf16[12,160,128]{2,1,0:T(8,128)(2,1)} %get-tuple-element.15.top_ref, bf16[12,160,128]{2,1,0:T(8,128)(2,1)} %get-tuple-element.16.bot_ref, bf16[12,96,128]{2,1,0:T(8,128)(2,1)} %get-tuple-element.17.left_ref, ...), custom_call_target="tpu_custom_call" | custom-call | tf_op jit(solution)/shard_map/conv1/pallas_call | solution.py:275
  336.1 34.9 %halo2.1 = (bf16[12,160,128]{2,1,0:T(8,128)(2,1)}, bf16[12,160,128]{2,1,0:T(8,128)(2,1)}, bf16[12,96,128]{2,1,0:T(8,128)(2,1)}, bf16[12,96,128]{2,1,0:T(8,128)(2,1)}) custom-call(s32[144]{0:T(256)} %reshape.83.tab_ref, bf16[12,64,128,128]{3,2,1,0:T(8,128)(2,1)} %bitcast.33, bf16[2,12,64,128]{3,2,1,0:T(8,128)(2,1)} %get-tuple-element.20.refs_1_), custom_call_target="tpu_custom_call" | custom-call | tf_op jit(solution)/shard_map/halo2/pallas_call | solution.py:441
  371.0 90.2 %conv2.1 = bf16[128,12,64,128]{3,2,1,0:T(8,128)(2,1)} custom-call(bf16[768,128,128]{2,1,0:T(8,128)(2,1)} %get-tuple-element.19.x_ref, bf16[12,160,128]{2,1,0:T(8,128)(2,1)} %get-tuple-element.21.top_ref, bf16[12,160,128]{2,1,0:T(8,128)(2,1)} %get-tuple-element.22.bot_ref, bf16[12,96,128]{2,1,0:T(8,128)(2,1)} %get-tuple-element.23.left_ref, ...), custom_call_target="tpu_custom_call" | custom-call | tf_op jit(solution)/shard_map/conv2/pallas_call | solution.py:275
  (32 shorter events, 3.3 us)
Async XLA Ops:
  2.0 7.3 %copy-start.2 = (s32[256]{0:T(256)}, s32[256]{0:T(256)S(1)}, u32[]{:S(2)}) copy-start(s32[256]{0:T(256)S(1)} %convert_add_fusion.pos_ref) | copy-start | bytes 3076
  2.9 22.6 %all-to-all-start = ((s32[32,1,24]{2,1,0:T(1,128)}), s32[32,1,24]{2,1,0:T(1,128)S(1)}, u32[]{:S(2)}, u32[]{:S(2)}) async-start(s32[32,1,24]{2,1,0:T(1,128)} %bitcast), calls=%async_computation | async-start | bytes 32768 | tf_op jit(solution)/shard_map/all_to_all | solution.py:493
  25.5 5.9 %copy-start.3 = (s32[12,4,3]{0,1,2:T(4,128)S(1)}, s32[12,4,3]{0,1,2:T(4,128)}, u32[]{:S(2)}) copy-start(s32[12,4,3]{0,1,2:T(4,128)} %param.14) | copy-start | bytes 1732
  25.5 6.8 %copy-start = (bf16[9,128,128]{2,1,0:T(8,128)(2,1)S(1)}, bf16[9,128,128]{2,1,0:T(8,128)(2,1)}, u32[]{:S(2)}) copy-start(bf16[9,128,128]{2,1,0:T(8,128)(2,1)} %param.17) | copy-start | bytes 884740
  25.5 7.6 %copy-start.4 = (f32[128]{0:T(128)S(1)}, f32[128]{0:T(128)}, u32[]{:S(2)}) copy-start(f32[128]{0:T(128)} %param.16) | copy-start | bytes 1540
  25.6 8.2 %copy-start.1 = (bf16[9,128,40]{1,2,0:T(8,128)(2,1)S(1)}, bf16[9,128,40]{1,2,0:T(8,128)(2,1)}, u32[]{:S(2)}) copy-start(bf16[9,128,40]{1,2,0:T(8,128)(2,1)} %param.15) | copy-start | bytes 276484
  25.6 177.6 %all-to-all-start.1 = ((bf16[32,24,40,128]{3,2,1,0:T(8,128)(2,1)}), bf16[32,24,40,128]{3,2,1,0:T(8,128)(2,1)}, u32[]{:S(2)}, u32[]{:S(2)}) async-start(bf16[32,24,40,128]{3,2,1,0:T(8,128)(2,1)} %bitcast.35), calls=%async_computation.1 | async-start | bytes 15728640 | tf_op jit(solution)/shard_map/all_to_all | solution.py:490

commit v2 on v1

--- a/solution.py
+++ b/solution.py
@@ -13,6 +13,9 @@
 PAIRS = 8
 UNROLLED = True
 CH = 16
+PLANES = 4
+ROUNDS = 2
+FAR_ORDER = (2, 1, 3)
 MESH = pl.DeviceIdType.MESH
 GELU_COEF = (
     0.7978842684146765,
@@ -70,6 +73,107 @@
         compiler_params=pltpu.CompilerParams(vmem_limit_bytes=VMEM_LIMIT),
         name="partials",
     )(position, source, weights)
+
+
+def route_kernel(caps, nb, nt, start_ref, out_ref, arr, *scratch):
+    kept = len(caps) * PLANES
+    packed, far_sem, near_sem, send_far, send_near = scratch[kept:]
+    held = [scratch[r * PLANES : (r + 1) * PLANES] for r in range(len(caps))]
+    members, each = packed.shape[2], packed.shape[3]
+    me = lax.axis_index("band") * nt + lax.axis_index("tile")
+    plane, place = me // members, me % members
+
+    def far_copy(r, off):
+        other = (plane + off) % PLANES
+        to = other * members + place
+        return pltpu.make_async_remote_copy(
+            src_ref=out_ref.at[r, other, pl.ds(0, caps[r])],
+            dst_ref=held[r][PLANES - off].at[pl.ds(0, caps[r])],
+            send_sem=send_far.at[r, off],
+            recv_sem=far_sem.at[r, PLANES - off],
+            device_id=(to // nt, to % nt),
+            device_id_type=MESH,
+        )
+
+    def own_copy(r):
+        return pltpu.make_async_copy(
+            out_ref.at[r, plane, pl.ds(0, caps[r])],
+            held[r][0].at[pl.ds(0, caps[r])],
+            far_sem.at[r, 0],
+        )
+
+    def near_copy(r, off, i):
+        to = plane * members + (place + i) % members
+        return pltpu.make_async_remote_copy(
+            src_ref=packed.at[r, off, i],
+            dst_ref=arr.at[r, off, (members - i) % members],
+            send_sem=send_near.at[r, off, i],
+            recv_sem=near_sem.at[r, off, (members - i) % members],
+            device_id=(to // nt, to % nt),
+            device_id_type=MESH,
+        )
+
+    def self_copy(r, off):
+        return pltpu.make_async_copy(packed.at[r, off, 0], arr.at[r, off, 0], near_sem.at[r, off, 0])
+
+    rounds = range(len(caps))
+    for r in rounds:
+        own_copy(r).start()
+    for r in rounds:
+        for off in FAR_ORDER:
+            far_copy(r, off).start()
+
+    def relay(r, off):
+        for i in range(members):
+            first = start_ref[((r * PLANES + off) * members) + i]
+            packed[r, off, i] = held[r][off][pl.ds(first, each)]
+            if i:
+                near_copy(r, off, i).start()
+            else:
+                self_copy(r, off).start()
+
+    for r in rounds:
+        own_copy(r).wait()
+        relay(r, 0)
+    for r in rounds:
+        for off in FAR_ORDER:
+            far_copy(r, PLANES - off).wait_recv()
+            relay(r, off)
+    for r in rounds:
+        for off in range(PLANES):
+            self_copy(r, off).wait()
+            for i in range(1, members):
+                near_copy(r, off, i).wait_send()
+                near_copy(r, off, members - i).wait_recv()
+    for r in rounds:
+        for off in FAR_ORDER:
+            far_copy(r, off).wait_send()
+
+
+def route(caps, starts, outgoing):
+    nb, nt = lax.axis_size("band"), lax.axis_size("tile")
+    rounds, _, most, fields, blk = outgoing.shape
+    members = nb * nt // PLANES
+    each = most // members
+    block = (fields, blk)
+    return pl.pallas_call(
+        functools.partial(route_kernel, caps, nb, nt),
+        out_shape=jax.ShapeDtypeStruct((rounds, PLANES, members, each) + block, BF),
+        in_specs=[pl.BlockSpec(memory_space=pltpu.SMEM), pl.BlockSpec(memory_space=pl.ANY)],
+        out_specs=pl.BlockSpec(memory_space=pl.ANY),
+        scratch_shapes=[pltpu.VMEM((c + each,) + block, BF) for c in caps for _ in range(PLANES)]
+        + [
+            pltpu.VMEM((rounds, PLANES, members, each) + block, BF),
+            pltpu.SemaphoreType.DMA((rounds, PLANES)),
+            pltpu.SemaphoreType.DMA((rounds, PLANES, members)),
+            pltpu.SemaphoreType.DMA((rounds, PLANES)),
+            pltpu.SemaphoreType.DMA((rounds, PLANES, members)),
+        ],
+        compiler_params=pltpu.CompilerParams(
+            has_side_effects=True, vmem_limit_bytes=VMEM_LIMIT
+        ),
+        name="route_packed" if caps[0] < most else "route_full",
+    )(starts, outgoing)
 
 
 def collect_kernel(slot_ref, arr_ref, out_ref, acc_ref):
@@ -482,16 +586,55 @@
     earlier = (jnp.arange(items)[:, None] > jnp.arange(items)[None, :]).astype(BF)
     before = jnp.dot(earlier, onehot.astype(BF), preferred_element_type=F32)
     rank_in = jnp.sum(before * onehot, axis=1).astype(jnp.int32)
-    position = target_dev * capacity + rank_in
-    hit = position[None, :] == jnp.arange(devices * capacity, dtype=jnp.int32)[:, None]
+    each = capacity // ROUNDS
+    members = devices // PLANES
+    most = members * each
+    slot_at = target_dev * capacity + rank_in
+    hit = slot_at[None, :] == jnp.arange(devices * capacity, dtype=jnp.int32)[:, None]
     out_slots = slots_dev + jnp.sum(jnp.where(hit, target_slot[None, :] - slots_dev, 0), axis=1)
-    outgoing = partials(position, source, regrid_weights, devices * capacity)
+
+    def parts_of(count):
+        r = jnp.arange(ROUNDS, dtype=jnp.int32).reshape((ROUNDS,) + (1,) * count.ndim)
+        part = jnp.clip(count[None] - r * each, 0, each)
+        part = part.reshape(part.shape[:-1] + (PLANES, members))
+        lower = jnp.arange(members)[:, None] < jnp.arange(members)[None, :]
+        before = jnp.sum(jnp.where(lower, part[..., :, None], 0), axis=-2)
+        return before, jnp.sum(part, axis=-1)
+
+    counts = jnp.sum(onehot, axis=0).astype(jnp.int32)
+    first = parts_of(counts)[0].reshape(ROUNDS * devices)
+    turn = rank_in // each
+    mine = (turn * devices + target_dev)[:, None] == jnp.arange(ROUNDS * devices)[None, :]
+    at = jnp.sum(jnp.where(mine, first[None, :], 0), axis=1)
+    position = (turn * PLANES + target_dev // members) * most + at + rank_in % each
+    outgoing = partials(position, source, regrid_weights, ROUNDS * PLANES * most)
     axes = ("band", "tile")
-    arrived = lax.all_to_all(
-        outgoing.reshape(devices, capacity, fields, block_len), axes, 0, 0, tiled=True
+    told = jnp.concatenate(
+        [out_slots.reshape(devices, capacity), jnp.broadcast_to(counts, (devices, devices))], axis=1
     )
-    arrived_slots = lax.all_to_all(
-        out_slots.reshape(devices, capacity), axes, 0, 0, tiled=True
+    told = lax.all_to_all(told, axes, 0, 0, tiled=True)
+    me = lax.axis_index("band") * nt + lax.axis_index("tile")
+    plane, place = me // members, me % members
+    starts, loads = parts_of(told[:, capacity:])
+    starts = starts.reshape(ROUNDS, PLANES, members, PLANES, members)
+    starts = lax.dynamic_slice(
+        starts, (0, 0, place, plane, 0), (ROUNDS, PLANES, 1, 1, members)
+    ).reshape(ROUNDS, PLANES, members)
+    near = (plane + jnp.arange(PLANES, dtype=jnp.int32)) % PLANES
+    there = (place + jnp.arange(members, dtype=jnp.int32)) % members
+    from_there = (place + jnp.arange(members, dtype=jnp.int32)) % members
+    starts = jnp.take(jnp.take(starts, near, axis=1), there, axis=2)
+    arrived_slots = told[:, :capacity].reshape(PLANES, members, ROUNDS, each)
+    arrived_slots = jnp.take(jnp.take(arrived_slots, near, axis=0), from_there, axis=1)
+    arrived_slots = arrived_slots.transpose(2, 0, 1, 3)
+    caps = (most * 5 // 6, most // 3)
+    fits = jnp.all(jnp.max(loads, axis=(1, 2)) <= jnp.array(caps, dtype=jnp.int32))
+    arrived = lax.cond(
+        fits,
+        functools.partial(route, caps),
+        functools.partial(route, (most,) * ROUNDS),
+        starts.reshape(-1),
+        outgoing.reshape(ROUNDS, PLANES, most, fields, block_len),
     )
     grid = collect(
         arrived_slots.reshape(-1), arrived.reshape(devices * capacity, fields, block_len), slots_dev

time: 462 us -> 442 us (0.957)
  waiting for transfers between devices: 166 us -> 0.01 us
  Pallas kernels: 264 us -> 406 us
  starting transfers between devices: 12.3 us -> 6.38 us
  local copies, waits for them, and re-layouts: 9.85 us -> 15.1 us
    all_to_all x2 -> x1, waiting for transfers between devices: 166 us -> 0.01 us  [local(): told = lax.all_to_all(told, axes, 0, 0, tiled=True)]
    pallas_call x0 -> x1, Pallas kernels: none -> 136 us  [route(): pl.pallas_call(functools.partial(route_kernel, caps, nb, nt), out_shape=j...]
    pallas_call x2, Pallas kernels: 77.7 us -> 83.7 us  [halo_exchange(): pl.pallas_call(functools.partial(halo_kernel, len(lines), nb, nt), out_sh...]
    all_to_all x2 -> x1, starting transfers between devices: 12.3 us -> 6.38 us  [local(): told = lax.all_to_all(told, axes, 0, 0, tiled=True)]
  transfers between devices with their start and end apart: 2 -> 1, of which waited for: 1 -> 0; matrix products, arithmetic and copies ran while one was open for 1% -> 2% of each run, Pallas kernels for 4% -> 4%
where the time goes in v2:
time: 442 us
  Pallas kernels  406 us (92%)
  local copies, waits for them, and re-layouts  15.1 us (3%)
  other arithmetic  7.02 us (2%)
  starting transfers between devices  6.38 us (1%)
  matrix products  5.59 us (1%)
    pallas_call x2, Pallas kernels, conv(): pl.pallas_call(functools.partial(conv_kernel, first), out_shape=out_shape...  156 us
    pallas_call x1, Pallas kernels, route(): pl.pallas_call(functools.partial(route_kernel, caps, nb, nt), out_shape=j...  136 us
    pallas_call x2, Pallas kernels, halo_exchange(): pl.pallas_call(functools.partial(halo_kernel, len(lines), nb, nt), out_sh...  83.7 us
    pallas_call x1, Pallas kernels, partials(): pl.pallas_call(partial_kernel, out_shape=jax.ShapeDtypeStruct((slots, fie...  16.4 us
    pallas_call x1, Pallas kernels, collect(): pl.pallas_call(collect_kernel, out_shape=jax.ShapeDtypeStruct((slots_dev,...  13.8 us
  transfers between devices with their start and end apart: 1, of which 0 were waited for; matrix products, arithmetic and copies ran while one was open for 2% of the time, Pallas kernels for 4%

profile of v2, /device:TPU:5, one launch (start us, length us, event | category | flops | bytes accessed | tf_op | source)
XLA Modules:
  0.0 441.6 jit_solution(14984122772162439988)
XLA Ops:
  0.0 0.8 copy.100
  4.2 6.4 %all-to-all-start = ((s32[32,1,56]{2,1,0:T(1,128)}), s32[32,1,56]{2,1,0:T(1,128)S(1)}, u32[]{:S(2)}, u32[]{:S(2)}) async-start(s32[32,1,56]{2,1,0:T(1,128)} %bitcast.14), calls=%async_computation | async-start | bytes 32768 | tf_op jit(solution)/shard_map/all_to_all | solution.py:615
  10.7 1.3 pad_maximum_fusion
  12.0 0.8 fusion.16
  12.8 1.2 copy.113
  14.1 0.7 fusion.12
  14.8 0.9 fusion.8
  15.7 0.8 copy.107
  16.5 0.7 reshape.281.tab_ref
  17.8 16.4 %partials.1 = bf16[768,40,128]{2,1,0:T(8,128)(2,1)} custom-call(s32[256]{0:T(256)} %get-tuple-element.311.pos_ref, bf16[40,8192]{1,0:T(8,128)(2,1)} %src_ref.1, bf16[64,4,128,128]{3,2,1,0:T(8,128)(2,1)} %w_ref.1), custom_call_target="tpu_custom_call" | custom-call | tf_op jit(solution)/shard_map/partials/pallas_call | solution.py:61
  34.5 0.7 compare_reduce_fusion
  38.1 138.9 %conditional.1 = (bf16[768,40,128]{2,1,0:T(8,128)(2,1)}) conditional(s32[]{:T(128)} %convert_element_type.47, (pred[8]{0:T(512)(128)(4,1)S(1)}, pred[4]{0:T(512)(128)(4,1)S(1)}, pred[8,8]{1,0:T(8,128)(4,1)S(1)}, s32[32,4,8]{0,2,1:T(8,128)S(1)}, s32[2]{0:T(128)S(1)}, /*index=5*/s32[]{:T(128)}, s32[]{:T(128)}, s32[4,1]{0,1:T(1,128)S(1)}, ...), branch_computations={%region_8.10_spmd, %region_10.12_spmd} | conditional | flops 36998 | bytes 58632 | solution.py:632
  40.8 136.1 %route_packed.2 = bf16[2,4,8,12,40,128]{5,4,3,2,1,0:T(8,128)(2,1)} custom-call(s32[64]{0:T(128)} %select_n.162.start_ref, bf16[2,4,96,40,128]{4,3,2,1,0:T(8,128)(2,1)} %bitcast.73), custom_call_target="tpu_custom_call" | custom-call | tf_op jit(solution)/shard_map/cond/branch_1_fun/route_packed/pallas_call | solution.py:159
  177.1 13.8 %collect.1.x_ref = bf16[768,40,128]{2,1,0:T(8,128)(2,1)} custom-call(s32[768]{0:T(1024)} %reshape.280.slot_ref, bf16[768,40,128]{2,1,0:T(8,128)(2,1)} %get-tuple-element.313.arr_ref), custom_call_target="tpu_custom_call" | custom-call | tf_op jit(solution)/shard_map/collect/pallas_call | solution.py:202
  190.9 5.4 %fusion.2 = bf16[2,768,40]{1,0,2:T(2,128)(2,1)S(1)} fusion(bf16[768,40,128]{2,1,0:T(8,128)(2,1)} %collect.1.x_ref, pred[2,128]{1,0:T(4,128)(4,1)S(1)} %gather_fusion.6), kind=kOutput, calls=%fused_computation.23 | convolution fusion | flops 15790080 | bytes 7987456 | tf_op jit(solution)/shard_map/ep,tcp->etc/dot_general | solution.py:644
  196.9 0.7 pad.25.refs_3_
  197.6 0.7 pad.24.refs_2_
  198.3 1.0 fusion.27
  199.5 0.8 pad.23.refs_1_
  200.6 0.8 pad.22.refs_0_
  201.4 48.9 %halo1.1 = (bf16[12,160,128]{2,1,0:T(8,128)(2,1)}, bf16[12,160,128]{2,1,0:T(8,128)(2,1)}, bf16[12,96,128]{2,1,0:T(8,128)(2,1)}, bf16[12,96,128]{2,1,0:T(8,128)(2,1)}) custom-call(s32[144]{0:T(256)} %reshape.281.tab_ref, bf16[12,128,128]{2,1,0:T(8,128)(2,1)} %pad.22.refs_0_, bf16[12,128,128]{2,1,0:T(8,128)(2,1)} %pad.23.refs_1_, ...), custom_call_target="tpu_custom_call" | custom-call | tf_op jit(solution)/shard_map/halo1/pallas_call | solution.py:545
  250.4 66.3 %conv1.1 = (bf16[768,128,128]{2,1,0:T(8,128)(2,1)}, bf16[2,12,64,128]{3,2,1,0:T(8,128)(2,1)}) custom-call(bf16[768,40,128]{2,1,0:T(8,128)(2,1)} %collect.1.x_ref, bf16[12,160,128]{2,1,0:T(8,128)(2,1)} %get-tuple-element.267.top_ref, bf16[12,160,128]{2,1,0:T(8,128)(2,1)} %get-tuple-element.268.bot_ref, bf16[12,96,128]{2,1,0:T(8,128)(2,1)} %get-tuple-element.269.left_ref, ...), custom_call_target="tpu_custom_call" | custom-call | tf_op jit(solution)/shard_map/conv1/pallas_call | solution.py:379
  316.6 34.8 %halo2.1 = (bf16[12,160,128]{2,1,0:T(8,128)(2,1)}, bf16[12,160,128]{2,1,0:T(8,128)(2,1)}, bf16[12,96,128]{2,1,0:T(8,128)(2,1)}, bf16[12,96,128]{2,1,0:T(8,128)(2,1)}) custom-call(s32[144]{0:T(256)} %reshape.281.tab_ref, bf16[12,64,128,128]{3,2,1,0:T(8,128)(2,1)} %bitcast.70, bf16[2,12,64,128]{3,2,1,0:T(8,128)(2,1)} %get-tuple-element.272.refs_1_), custom_call_target="tpu_custom_call" | custom-call | tf_op jit(solution)/shard_map/halo2/pallas_call | solution.py:545
  351.4 90.2 %conv2.1 = bf16[128,12,64,128]{3,2,1,0:T(8,128)(2,1)} custom-call(bf16[768,128,128]{2,1,0:T(8,128)(2,1)} %get-tuple-element.271.x_ref, bf16[12,160,128]{2,1,0:T(8,128)(2,1)} %get-tuple-element.273.top_ref, bf16[12,160,128]{2,1,0:T(8,128)(2,1)} %get-tuple-element.274.bot_ref, bf16[12,96,128]{2,1,0:T(8,128)(2,1)} %get-tuple-element.275.left_ref, ...), custom_call_target="tpu_custom_call" | custom-call | tf_op jit(solution)/shard_map/conv2/pallas_call | solution.py:379
  (71 shorter events, 10.3 us)
Async XLA Ops:
  4.2 30.0 %all-to-all-start = ((s32[32,1,56]{2,1,0:T(1,128)}), s32[32,1,56]{2,1,0:T(1,128)S(1)}, u32[]{:S(2)}, u32[]{:S(2)}) async-start(s32[32,1,56]{2,1,0:T(1,128)} %bitcast.14), calls=%async_computation | async-start | bytes 32768 | tf_op jit(solution)/shard_map/all_to_all | solution.py:615
  17.8 16.7 %copy-start = (s32[2]{0:T(128)S(1)}, s32[2]{0:T(128)}, u32[]{:S(2)}) copy-start(s32[2]{0:T(128)} %constant.185.clone) | copy-start | bytes 28

commit v3 on v2

--- a/solution.py
+++ b/solution.py
@@ -11,7 +11,7 @@
 F32 = jnp.float32
 VMEM_LIMIT = 60 * 1024 * 1024
 PAIRS = 8
-UNROLLED = True
+PIECES = 2
 CH = 16
 PLANES = 4
 ROUNDS = 2
@@ -29,13 +29,13 @@
 GELU_CAP = 30.0
 
 
-def gelu(v):
-    u = jnp.minimum(v * v, GELU_CAP)
-    q = jnp.full_like(u, GELU_COEF[-1])
-    for c in GELU_COEF[-2::-1]:
+def gelu_of_half(h):
+    u = jnp.minimum(h * h, 0.25 * GELU_CAP)
+    coefs = [2.0 * 4.0**i * c for i, c in enumerate(GELU_COEF)]
+    q = coefs[-1] * u + coefs[-2]
+    for c in coefs[-3::-1]:
         q = q * u + c
-    half = 0.5 * v
-    return half + half * jnp.tanh(v * q)
+    return h + h * jnp.tanh(h * q)
 
 
 def partial_kernel(pos_ref, src_ref, w_ref, out_ref):
@@ -57,7 +57,7 @@
 def partials(position, source, weights, slots):
     fields = source.shape[0]
     src_count, top, blk, _ = weights.shape
-    step = 4
+    step = min(16, src_count)
     return pl.pallas_call(
         partial_kernel,
         out_shape=jax.ShapeDtypeStruct((slots, fields, blk), BF),
@@ -215,7 +215,7 @@
 
 
 def conv_kernel(
-    first, x_ref, top_ref, bot_ref, left_ref, right_ref, wa_ref, wb_ref, b_ref, out_ref, *scratch
+    first, x_ref, top_ref, bot_ref, left_ref, right_ref, w_ref, b_ref, out_ref, *scratch
 ):
     if first:
         ends_ref, ends = scratch[0], scratch[-1]
@@ -269,68 +269,56 @@
     put(0, 0, 0, row, lo, hi)
     row, lo, hi = halo_row(bot_ref)
     put(1, rows // 2, 1, row, lo, hi)
-    unroll = UNROLLED
     n = 2 * PAIRS
-
-    def fill_loop(i, _):
-        for k in range(slots):
-            put_row(i * slots + k, k)
-        return 0
-
-    def dots(p0):
-        a = sl[pl.ds(p0, PAIRS)].reshape(PAIRS * cols, 2 * width)
-        b = sl[pl.ds(p0 + 1, PAIRS)].reshape(PAIRS * cols, 2 * width)
-        return jnp.dot(a, wa_ref[...], preferred_element_type=F32) + jnp.dot(
-            b, wb_ref[...], preferred_element_type=F32
-        )
-
-    def finish(g, y):
-        p0 = g * PAIRS
-        hid = y.shape[1] // 2
+    chunks = rows // n
+    hid = w_ref.shape[1] // 2
+    held = scratch[3]
+
+    per = PAIRS // PIECES
+
+    def dots(g, piece):
+        p0 = piece * per
+        a = sl[pl.ds(g * PAIRS + p0, per)].reshape(per * cols, 2 * width)
+        b = sl[pl.ds(g * PAIRS + p0 + 1, per)].reshape(per * cols, 2 * width)
+        y = jnp.dot(
+            jnp.concatenate([a, b], axis=1), w_ref[...], preferred_element_type=F32
+        )
         if first:
-            y = gelu(y + b_ref[...])
-            for p in range(PAIRS):
+            held[g % 2, p0 * cols : (p0 + per) * cols, :] = y
+            return
+        for p in range(per):
+            for q in range(2):
+                part = y[p * cols : (p + 1) * cols, q * hid : (q + 1) * hid]
+                held[g % 2, pl.ds(2 * (p0 + p) + q, hid, stride=n), :] = part.T
+
+    def finish(g, piece):
+        slot = g % 2
+        if first:
+            for p in range(piece * per, (piece + 1) * per):
+                y = gelu_of_half(held[slot, p * cols : (p + 1) * cols, :] + b_ref[...])
                 for q in range(2):
-                    part = y[p * cols : (p + 1) * cols, q * hid : (q + 1) * hid].astype(BF)
-                    r = 2 * (p0 + p) + q
+                    part = y[:, q * hid : (q + 1) * hid].astype(BF)
+                    r = 2 * (g * PAIRS + p) + q
                     out_ref[r] = part
                     ends[0, pl.ds(r, 1), :] = part[:1].astype(F32)
                     ends[1, pl.ds(r, 1), :] = part[cols - 1 :].astype(F32)
             return
-        flip = scratch[3].at[g % 2 if unroll else 0]
-        for p in range(PAIRS):
-            for q in range(2):
-                part = y[p * cols : (p + 1) * cols, q * hid : (q + 1) * hid]
-                flip[pl.ds(2 * p + q, hid, stride=n), :] = part.T
-
-        def group(o, _):
-            for j in range(8):
-                v = flip[pl.ds((o * 8 + j) * n, n), :]
-                out_ref[o * 8 + j, 0, pl.ds(g * n, n), :] = gelu(v + b_ref[o * 8 + j]).astype(BF)
-            return 0
-
-        if unroll:
-            for o in range(hid // 8):
-                group(o, 0)
-        else:
-            lax.fori_loop(0, hid // 8, group, 0)
-
-    if unroll:
-        for k in range(min(n + 2, rows)):
+        for o in range(hid * piece // PIECES, hid * (piece + 1) // PIECES):
+            v = held[slot, o * n : (o + 1) * n, :]
+            out_ref[o, 0, g * n : (g + 1) * n, :] = gelu_of_half(v + b_ref[o]).astype(BF)
+
+    def put_for(g, piece):
+        lo = g * n + 2 + piece * 2 * per if g or piece else 0
+        for k in range(lo, min(g * n + 2 + (piece + 1) * 2 * per, rows)):
             put_row(k, k)
-        for g in range(rows // n):
-            y = dots(g * PAIRS)
-            for k in range((g + 1) * n + 2, min((g + 2) * n + 2, rows)):
-                put_row(k, k)
-            finish(g, y)
-    else:
-        lax.fori_loop(0, rows // slots, fill_loop, 0)
-
-        def chunk(g, _):
-            finish(g, dots(g * PAIRS))
-            return 0
-
-        lax.fori_loop(0, rows // n, chunk, 0)
+
+    for g in range(chunks + 1):
+        for piece in range(PIECES):
+            if g < chunks:
+                put_for(g, piece)
+                dots(g, piece)
+            if g:
+                finish(g - 1, piece)
     if first:
         ends_ref[:, 0] = ends[...].astype(BF)
 
@@ -351,8 +339,8 @@
         jnp.concatenate([w[a] if a < 3 else zero, w[a - 1] if a > 0 else zero], axis=1)
         for a in range(4)
     ]
-    wa = jnp.concatenate(wide[:2], axis=0)
-    wb = jnp.concatenate(wide[2:], axis=0)
+    w = jnp.concatenate(wide, axis=0) * 0.5
+    bias = bias * 0.5
     scratch = [
         pltpu.VMEM((rows // 2 + 1, cols, 2 * width), BF),
         pltpu.VMEM((8, cols + 16, cols), F32),
@@ -369,6 +357,7 @@
             pl.BlockSpec((rows, cols, hid), lambda f: (f, 0, 0)),
             pl.BlockSpec((2, 1, rows, hid), lambda f: (0, f, 0, 0)),
         )
+        scratch.append(pltpu.VMEM((2, PAIRS * cols, 2 * hid), F32))
         scratch.append(pltpu.VMEM((2, rows, hid), F32))
     else:
         bias_in = bias
@@ -386,15 +375,14 @@
             pl.BlockSpec((1,) + bot.shape[1:], lambda f: (f, 0, 0)),
             pl.BlockSpec((1,) + left.shape[1:], lambda f: (f, 0, 0)),
             pl.BlockSpec((1,) + right.shape[1:], lambda f: (f, 0, 0)),
-            pl.BlockSpec(wa.shape, lambda f: (0, 0)),
-            pl.BlockSpec(wb.shape, lambda f: (0, 0)),
+            pl.BlockSpec(w.shape, lambda f: (0, 0)),
             bias_spec,
         ],
         out_specs=out_spec,
         scratch_shapes=scratch,
         compiler_params=pltpu.CompilerParams(vmem_limit_bytes=VMEM_LIMIT),
         name="conv1" if first else "conv2",
-    )(x, top, bot, left, right, wa, wb, bias_in)
+    )(x, top, bot, left, right, w, bias_in)
 
 
 def halo_kernel(line_refs, nb, nt, tab_ref, *refs):

time: 442 us -> 426 us (0.964)
  Pallas kernels: 406 us -> 390 us
    pallas_call x2, Pallas kernels: 156 us -> 146 us  [conv(): pl.pallas_call(functools.partial(conv_kernel, first), out_shape=out_shape...]
    pallas_call x1, Pallas kernels: 16.4 us -> 10.7 us  [partials(): pl.pallas_call(partial_kernel, out_shape=jax.ShapeDtypeStruct((slots, fie...]
  transfers between devices with their start and end apart: 1 -> 1, of which waited for: 0 -> 0; matrix products, arithmetic and copies ran while one was open for 2% -> 2% of each run, Pallas kernels for 4% -> 3%
where the time goes in v3:
time: 426 us
  Pallas kernels  390 us (92%)
  local copies, waits for them, and re-layouts  14.4 us (3%)
  other arithmetic  8.25 us (2%)
  starting transfers between devices  6.38 us (1%)
  matrix products  5.59 us (1%)
    pallas_call x2, Pallas kernels, conv(): pl.pallas_call(functools.partial(conv_kernel, first), out_shape=out_shape...  146 us
    pallas_call x1, Pallas kernels, route(): pl.pallas_call(functools.partial(route_kernel, caps, nb, nt), out_shape=j...  136 us
    pallas_call x2, Pallas kernels, halo_exchange(): pl.pallas_call(functools.partial(halo_kernel, len(lines), nb, nt), out_sh...  83.5 us
    pallas_call x1, Pallas kernels, collect(): pl.pallas_call(collect_kernel, out_shape=jax.ShapeDtypeStruct((slots_dev,...  13.8 us
    pallas_call x1, Pallas kernels, partials(): pl.pallas_call(partial_kernel, out_shape=jax.ShapeDtypeStruct((slots, fie...  10.7 us
  transfers between devices with their start and end apart: 1, of which 0 were waited for; matrix products, arithmetic and copies ran while one was open for 2% of the time, Pallas kernels for 3%

profile of v3, /device:TPU:5, one launch (start us, length us, event | category | flops | bytes accessed | tf_op | source)
XLA Modules:
  0.0 425.7 jit_solution(14375408078986737714)
XLA Ops:
  0.0 0.8 copy.100
  1.2 0.7 broadcast_add_fusion.1
  4.1 6.4 %all-to-all-start = ((s32[32,1,56]{2,1,0:T(1,128)}), s32[32,1,56]{2,1,0:T(1,128)S(1)}, u32[]{:S(2)}, u32[]{:S(2)}) async-start(s32[32,1,56]{2,1,0:T(1,128)} %bitcast.14), calls=%async_computation | async-start | bytes 32768 | tf_op jit(solution)/shard_map/all_to_all | solution.py:603
  11.9 1.2 broadcast_multiply_fusion.b_ref
  13.2 0.8 fusion.19
  14.0 1.2 copy.113
  15.2 0.7 fusion.15.w_ref
  15.9 1.1 fusion.9.w_ref
  17.1 0.7 reshape.281.tab_ref
  18.4 10.7 %partials.1 = bf16[768,40,128]{2,1,0:T(8,128)(2,1)} custom-call(s32[256]{0:T(256)} %get-tuple-element.307.pos_ref, bf16[40,8192]{1,0:T(8,128)(2,1)} %src_ref.1, bf16[64,4,128,128]{3,2,1,0:T(8,128)(2,1)} %w_ref.1), custom_call_target="tpu_custom_call" | custom-call | tf_op jit(solution)/shard_map/partials/pallas_call | solution.py:61
  32.2 0.7 reshape.280.slot_ref
  32.9 138.9 %conditional.1 = (bf16[768,40,128]{2,1,0:T(8,128)(2,1)}) conditional(s32[]{:T(128)} %convert_element_type.47, (pred[8]{0:T(512)(128)(4,1)S(1)}, pred[4]{0:T(512)(128)(4,1)S(1)}, pred[8,8]{1,0:T(8,128)(4,1)S(1)}, s32[32,4,8]{0,2,1:T(8,128)S(1)}, s32[2]{0:T(128)S(1)}, /*index=5*/s32[]{:T(128)}, s32[]{:T(128)}, s32[4,1]{0,1:T(1,128)S(1)}, ...), branch_computations={%region_8.10_spmd, %region_10.12_spmd} | conditional | flops 36998 | bytes 58632 | solution.py:620
  35.5 136.1 %route_packed.2 = bf16[2,4,8,12,40,128]{5,4,3,2,1,0:T(8,128)(2,1)} custom-call(s32[64]{0:T(128)} %select_n.162.start_ref, bf16[2,4,96,40,128]{4,3,2,1,0:T(8,128)(2,1)} %bitcast.73), custom_call_target="tpu_custom_call" | custom-call | tf_op jit(solution)/shard_map/cond/branch_1_fun/route_packed/pallas_call | solution.py:159
  171.8 13.8 %collect.1.x_ref = bf16[768,40,128]{2,1,0:T(8,128)(2,1)} custom-call(s32[768]{0:T(1024)} %reshape.280.slot_ref, bf16[768,40,128]{2,1,0:T(8,128)(2,1)} %get-tuple-element.309.arr_ref), custom_call_target="tpu_custom_call" | custom-call | tf_op jit(solution)/shard_map/collect/pallas_call | solution.py:202
  185.6 5.4 %fusion.4 = bf16[2,768,40]{1,0,2:T(2,128)(2,1)S(1)} fusion(bf16[768,40,128]{2,1,0:T(8,128)(2,1)} %collect.1.x_ref, pred[2,128]{1,0:T(4,128)(4,1)S(1)} %gather_fusion.6), kind=kOutput, calls=%fused_computation.27 | convolution fusion | flops 15790080 | bytes 7987456 | tf_op jit(solution)/shard_map/ep,tcp->etc/dot_general | solution.py:632
  191.6 0.7 pad.25.refs_3_
  192.3 0.7 pad.24.refs_2_
  193.0 1.0 fusion.31
  194.2 0.8 pad.23.refs_1_
  195.3 0.8 pad.22.refs_0_
  196.2 48.8 %halo1.1 = (bf16[12,160,128]{2,1,0:T(8,128)(2,1)}, bf16[12,160,128]{2,1,0:T(8,128)(2,1)}, bf16[12,96,128]{2,1,0:T(8,128)(2,1)}, bf16[12,96,128]{2,1,0:T(8,128)(2,1)}) custom-call(s32[144]{0:T(256)} %reshape.281.tab_ref, bf16[12,128,128]{2,1,0:T(8,128)(2,1)} %pad.22.refs_0_, bf16[12,128,128]{2,1,0:T(8,128)(2,1)} %pad.23.refs_1_, ...), custom_call_target="tpu_custom_call" | custom-call | tf_op jit(solution)/shard_map/halo1/pallas_call | solution.py:533
  245.0 58.6 %conv1.1 = (bf16[768,128,128]{2,1,0:T(8,128)(2,1)}, bf16[2,12,64,128]{3,2,1,0:T(8,128)(2,1)}) custom-call(bf16[768,40,128]{2,1,0:T(8,128)(2,1)} %collect.1.x_ref, bf16[12,160,128]{2,1,0:T(8,128)(2,1)} %get-tuple-element.267.top_ref, bf16[12,160,128]{2,1,0:T(8,128)(2,1)} %get-tuple-element.268.bot_ref, bf16[12,96,128]{2,1,0:T(8,128)(2,1)} %get-tuple-element.269.left_ref, ...), custom_call_target="tpu_custom_call" | custom-call | tf_op jit(solution)/shard_map/conv1/pallas_call | solution.py:368
  303.6 34.7 %halo2.1 = (bf16[12,160,128]{2,1,0:T(8,128)(2,1)}, bf16[12,160,128]{2,1,0:T(8,128)(2,1)}, bf16[12,96,128]{2,1,0:T(8,128)(2,1)}, bf16[12,96,128]{2,1,0:T(8,128)(2,1)}) custom-call(s32[144]{0:T(256)} %reshape.281.tab_ref, bf16[12,64,128,128]{3,2,1,0:T(8,128)(2,1)} %bitcast.70, bf16[2,12,64,128]{3,2,1,0:T(8,128)(2,1)} %get-tuple-element.272.refs_1_), custom_call_target="tpu_custom_call" | custom-call | tf_op jit(solution)/shard_map/halo2/pallas_call | solution.py:533
  338.3 87.3 %conv2.1 = bf16[128,12,64,128]{3,2,1,0:T(8,128)(2,1)} custom-call(bf16[768,128,128]{2,1,0:T(8,128)(2,1)} %get-tuple-element.271.x_ref, bf16[12,160,128]{2,1,0:T(8,128)(2,1)} %get-tuple-element.273.top_ref, bf16[12,160,128]{2,1,0:T(8,128)(2,1)} %get-tuple-element.274.bot_ref, bf16[12,96,128]{2,1,0:T(8,128)(2,1)} %get-tuple-element.275.left_ref, ...), custom_call_target="tpu_custom_call" | custom-call | tf_op jit(solution)/shard_map/conv2/pallas_call | solution.py:368
  (75 shorter events, 10.9 us)
Async XLA Ops:
  1.9 15.1 %copy-start = (s32[12,4,3]{0,1,2:T(4,128)S(1)}, s32[12,4,3]{0,1,2:T(4,128)}, u32[]{:S(2)}) copy-start(s32[12,4,3]{0,1,2:T(4,128)} %param.17) | copy-start | bytes 1732
  4.1 24.9 %all-to-all-start = ((s32[32,1,56]{2,1,0:T(1,128)}), s32[32,1,56]{2,1,0:T(1,128)S(1)}, u32[]{:S(2)}, u32[]{:S(2)}) async-start(s32[32,1,56]{2,1,0:T(1,128)} %bitcast.14), calls=%async_computation | async-start | bytes 32768 | tf_op jit(solution)/shard_map/all_to_all | solution.py:603
  18.4 11.0 %copy-start.1 = (s32[2]{0:T(128)S(1)}, s32[2]{0:T(128)}, u32[]{:S(2)}) copy-start(s32[2]{0:T(128)} %constant.190.clone) | copy-start | bytes 28

commit v4 on v3

--- a/solution.py
+++ b/solution.py
@@ -172,7 +172,7 @@
         compiler_params=pltpu.CompilerParams(
             has_side_effects=True, vmem_limit_bytes=VMEM_LIMIT
         ),
-        name="route_packed" if caps[0] < most else "route_full",
+        name="route_" + "_".join(map(str, caps)),
     )(starts, outgoing)
 
 
@@ -615,12 +615,12 @@
     arrived_slots = told[:, :capacity].reshape(PLANES, members, ROUNDS, each)
     arrived_slots = jnp.take(jnp.take(arrived_slots, near, axis=0), from_there, axis=1)
     arrived_slots = arrived_slots.transpose(2, 0, 1, 3)
-    caps = (most * 5 // 6, most // 3)
-    fits = jnp.all(jnp.max(loads, axis=(1, 2)) <= jnp.array(caps, dtype=jnp.int32))
-    arrived = lax.cond(
-        fits,
-        functools.partial(route, caps),
-        functools.partial(route, (most,) * ROUNDS),
+    peak = jnp.max(loads, axis=(1, 2))
+    levels = [(most * 5 // 6, most // 4), (most * 5 // 6, most // 3), (most,) * ROUNDS]
+    fit = [jnp.all(peak <= jnp.array(caps, dtype=jnp.int32)) for caps in levels[:-1]]
+    arrived = lax.switch(
+        jnp.where(fit[0], 0, jnp.where(fit[1], 1, 2)),
+        [functools.partial(route, caps) for caps in levels],
         starts.reshape(-1),
         outgoing.reshape(ROUNDS, PLANES, most, fields, block_len),
     )

time: 426 us -> 424 us (level)
    pallas_call x1, Pallas kernels: 136 us -> 131 us  [route(): pl.pallas_call(functools.partial(route_kernel, caps, nb, nt), out_shape=j...]
where the time goes in v4:
time: 424 us; the launch traced here: 423 us
  Pallas kernels  387 us (91%)
  local copies, waits for them, and re-layouts  14.4 us (3%)
  other arithmetic  8.25 us (2%)
  starting transfers between devices  6.38 us (2%)
  matrix products  5.59 us (1%)
    pallas_call x2, Pallas kernels, conv(): pl.pallas_call(functools.partial(conv_kernel, first), out_shape=out_shape...  146 us
    pallas_call x1, Pallas kernels, route(): pl.pallas_call(functools.partial(route_kernel, caps, nb, nt), out_shape=j...  131 us
    pallas_call x2, Pallas kernels, halo_exchange(): pl.pallas_call(functools.partial(halo_kernel, len(lines), nb, nt), out_sh...  85.2 us
    pallas_call x1, Pallas kernels, collect(): pl.pallas_call(collect_kernel, out_shape=jax.ShapeDtypeStruct((slots_dev,...  13.9 us
    pallas_call x1, Pallas kernels, partials(): pl.pallas_call(partial_kernel, out_shape=jax.ShapeDtypeStruct((slots, fie...  10.6 us
  transfers between devices with their start and end apart: 1, of which 0 were waited for; matrix products, arithmetic and copies ran while one was open for 2% of the time, Pallas kernels for 3%

profile of v4, /device:TPU:5, one launch (start us, length us, event | category | flops | bytes accessed | tf_op | source)
XLA Modules:
  0.0 422.8 jit_solution(15988829054253354150)
XLA Ops:
  0.0 0.8 copy.122
  1.2 0.7 broadcast_add_fusion.1
  4.1 6.4 %all-to-all-start = ((s32[32,1,56]{2,1,0:T(1,128)}), s32[32,1,56]{2,1,0:T(1,128)S(1)}, u32[]{:S(2)}, u32[]{:S(2)}) async-start(s32[32,1,56]{2,1,0:T(1,128)} %bitcast.21), calls=%async_computation | async-start | bytes 32768 | tf_op jit(solution)/shard_map/all_to_all | solution.py:603
  11.9 1.2 broadcast_multiply_fusion.b_ref
  13.2 0.8 fusion.19
  14.0 1.2 copy.135
  15.2 0.7 fusion.15.w_ref
  15.9 1.1 fusion.9.w_ref
  17.1 0.7 reshape.303.tab_ref
  18.4 10.6 %partials.1 = bf16[768,40,128]{2,1,0:T(8,128)(2,1)} custom-call(s32[256]{0:T(256)} %get-tuple-element.444.pos_ref, bf16[40,8192]{1,0:T(8,128)(2,1)} %src_ref.1, bf16[64,4,128,128]{3,2,1,0:T(8,128)(2,1)} %w_ref.1), custom_call_target="tpu_custom_call" | custom-call | tf_op jit(solution)/shard_map/partials/pallas_call | solution.py:61
  32.8 0.7 reshape.302.slot_ref
  33.5 133.7 %conditional.1 = (bf16[768,40,128]{2,1,0:T(8,128)(2,1)}) conditional(s32[]{:T(128)} %clamp.26, (pred[8]{0:T(512)(128)(4,1)S(1)}, pred[4]{0:T(512)(128)(4,1)S(1)}, pred[8,8]{1,0:T(8,128)(4,1)S(1)}, s32[32,4,8]{0,2,1:T(8,128)S(1)}, s32[2]{0:T(128)S(1)}, /*index=5*/s32[]{:T(128)}, s32[]{:T(128)}, s32[4,1]{0,1:T(1,128)S(1)}, ...), branch_computations={%region_9.11_spmd, %region_11.13_spmd, %region_13.15_spmd} | conditional | flops 36998 | bytes 58632 | solution.py:621
  36.1 130.8 %route_80_24.2 = bf16[2,4,8,12,40,128]{5,4,3,2,1,0:T(8,128)(2,1)} custom-call(s32[64]{0:T(128)} %select_n.179.start_ref, bf16[2,4,96,40,128]{4,3,2,1,0:T(8,128)(2,1)} %bitcast.83), custom_call_target="tpu_custom_call" | custom-call | tf_op jit(solution)/shard_map/cond/branch_0_fun/route_80_24/pallas_call | solution.py:159
  167.2 13.9 %collect.1.x_ref = bf16[768,40,128]{2,1,0:T(8,128)(2,1)} custom-call(s32[768]{0:T(1024)} %reshape.302.slot_ref, bf16[768,40,128]{2,1,0:T(8,128)(2,1)} %get-tuple-element.446.arr_ref), custom_call_target="tpu_custom_call" | custom-call | tf_op jit(solution)/shard_map/collect/pallas_call | solution.py:202
  181.1 5.4 %fusion.4 = bf16[2,768,40]{1,0,2:T(2,128)(2,1)S(1)} fusion(bf16[768,40,128]{2,1,0:T(8,128)(2,1)} %collect.1.x_ref, pred[2,128]{1,0:T(4,128)(4,1)S(1)} %gather_fusion.8), kind=kOutput, calls=%fused_computation.36 | convolution fusion | flops 15790080 | bytes 7987456 | tf_op jit(solution)/shard_map/ep,tcp->etc/dot_general | solution.py:632
  187.0 0.7 pad.25.refs_3_
  187.8 0.7 pad.24.refs_2_
  188.5 1.0 fusion.31
  189.7 0.8 pad.23.refs_1_
  190.8 0.8 pad.22.refs_0_
  191.6 50.5 %halo1.1 = (bf16[12,160,128]{2,1,0:T(8,128)(2,1)}, bf16[12,160,128]{2,1,0:T(8,128)(2,1)}, bf16[12,96,128]{2,1,0:T(8,128)(2,1)}, bf16[12,96,128]{2,1,0:T(8,128)(2,1)}) custom-call(s32[144]{0:T(256)} %reshape.303.tab_ref, bf16[12,128,128]{2,1,0:T(8,128)(2,1)} %pad.22.refs_0_, bf16[12,128,128]{2,1,0:T(8,128)(2,1)} %pad.23.refs_1_, ...), custom_call_target="tpu_custom_call" | custom-call | tf_op jit(solution)/shard_map/halo1/pallas_call | solution.py:533
  242.1 58.6 %conv1.1 = (bf16[768,128,128]{2,1,0:T(8,128)(2,1)}, bf16[2,12,64,128]{3,2,1,0:T(8,128)(2,1)}) custom-call(bf16[768,40,128]{2,1,0:T(8,128)(2,1)} %collect.1.x_ref, bf16[12,160,128]{2,1,0:T(8,128)(2,1)} %get-tuple-element.392.top_ref, bf16[12,160,128]{2,1,0:T(8,128)(2,1)} %get-tuple-element.393.bot_ref, bf16[12,96,128]{2,1,0:T(8,128)(2,1)} %get-tuple-element.394.left_ref, ...), custom_call_target="tpu_custom_call" | custom-call | tf_op jit(solution)/shard_map/conv1/pallas_call | solution.py:368
  300.8 34.7 %halo2.1 = (bf16[12,160,128]{2,1,0:T(8,128)(2,1)}, bf16[12,160,128]{2,1,0:T(8,128)(2,1)}, bf16[12,96,128]{2,1,0:T(8,128)(2,1)}, bf16[12,96,128]{2,1,0:T(8,128)(2,1)}) custom-call(s32[144]{0:T(256)} %reshape.303.tab_ref, bf16[12,64,128,128]{3,2,1,0:T(8,128)(2,1)} %bitcast.86, bf16[2,12,64,128]{3,2,1,0:T(8,128)(2,1)} %get-tuple-element.397.refs_1_), custom_call_target="tpu_custom_call" | custom-call | tf_op jit(solution)/shard_map/halo2/pallas_call | solution.py:533
  335.5 87.3 %conv2.1 = bf16[128,12,64,128]{3,2,1,0:T(8,128)(2,1)} custom-call(bf16[768,128,128]{2,1,0:T(8,128)(2,1)} %get-tuple-element.396.x_ref, bf16[12,160,128]{2,1,0:T(8,128)(2,1)} %get-tuple-element.398.top_ref, bf16[12,160,128]{2,1,0:T(8,128)(2,1)} %get-tuple-element.399.bot_ref, bf16[12,96,128]{2,1,0:T(8,128)(2,1)} %get-tuple-element.400.left_ref, ...), custom_call_target="tpu_custom_call" | custom-call | tf_op jit(solution)/shard_map/conv2/pallas_call | solution.py:368
  (77 shorter events, 10.9 us)
Async XLA Ops:
  1.9 15.1 %copy-start = (s32[12,4,3]{0,1,2:T(4,128)S(1)}, s32[12,4,3]{0,1,2:T(4,128)}, u32[]{:S(2)}) copy-start(s32[12,4,3]{0,1,2:T(4,128)} %param.19) | copy-start | bytes 1732
  4.1 24.9 %all-to-all-start = ((s32[32,1,56]{2,1,0:T(1,128)}), s32[32,1,56]{2,1,0:T(1,128)S(1)}, u32[]{:S(2)}, u32[]{:S(2)}) async-start(s32[32,1,56]{2,1,0:T(1,128)} %bitcast.21), calls=%async_computation | async-start | bytes 32768 | tf_op jit(solution)/shard_map/all_to_all | solution.py:603
  18.4 11.0 %copy-start.1 = (s32[2]{0:T(128)S(1)}, s32[2]{0:T(128)}, u32[]{:S(2)}) copy-start(s32[2]{0:T(128)} %constant.204.clone) | copy-start | bytes 28
  18.4 11.0 %copy-start.2 = (s32[2]{0:T(128)S(1)}, s32[2]{0:T(128)}, u32[]{:S(2)}) copy-start(s32[2]{0:T(128)} %constant.203.clone) | copy-start | bytes 28
